TPU v7x, 256 devices: a whole 4x4x8 slice. The times are simulated.
256 devices in a mesh: dom: 256 (over y, x, z, core).
Axes of the slice: x: 4, y: 4, z: 8, core: 2. Of those that a mesh axis runs over, the one named last changes fastest.
Arguments:
- rhs: float32 [8, 1703936], P(None, 'dom'), may hold values from -25 to 25, as said below
- potential: float32 [1703936], P('dom'), may hold values from 0.5 to 2
- precond: float32 [1703936], P('dom'), may hold values from 0.05 to 0.5
- shift: float32 [8], replicated, may hold values from 0.3 to 3
- stiffness: float32 [343, 343], replicated, may hold values from -0.4 to 2, as said below
- cell_scale: float32 [8192], P('dom'), may hold values from 0.5 to 2
- conn: int32 [8192, 343], P('dom'), may hold values from 0 to 7487, as said below
- cell_count: int32 [256], replicated, may hold values from 1 to 32, as said below
- projector: float32 [2048, 8, 343], P('dom'), may hold values from -0.6 to 0.6
- support_cell: int32 [2048], P('dom'), may hold values from 0 to 31, as said below
- support_atom: int32 [2048], P('dom'), may hold values from 0 to 511, as said below
- support_count: int32 [256], replicated, may hold values from 4 to 8, as said below
- atom_matrix: float32 [512, 8, 8], P('dom'), may hold values from -2 to 15, as said below
Outputs:
- solution: float32 [8, 1703936], P(None, 'dom')
- residual: float32 [8, 1703936], P(None, 'dom')
Inputs may be any that keep to these rules, and one draw needn't show every extreme that they name: `rhs`: row v rises in scale along the nodes. `stiffness`: symmetric positive definite. `atom_matrix`: each atom's matrix is symmetric positive definite. Block b's live cells are its slots 0 to cell_count[b] - 1; blocks 2k and 2k + 1 together hold at most 40 live cells, and some block holds 32. `conn`: a local index i of block b is column b * 6656 + i of the field padded by 416 zero columns at each end: indices below 416 are the previous block's last nodes, indices from 7072 on the next block's first nodes. `support_cell`: every entry names a live cell of its block. `support_atom`: atom a is owned by block a // 2; an entry of block b names an atom owned by block b - 1, b or b + 1. Block b's live entries are its first support_count[b]; some block has 8.
All inputs are finite; a program needn't handle non-finite values.
Results may differ from a plain program's by a relative error of at most 0.0003.
Values sent between devices are 32-bit elements; how exact they have to be, the bound alone decides.
A program may use at most 64 MiB of HBM per device.

v0:
```python
import functools

import jax
import jax.numpy as jnp
from jax import lax
from jax.sharding import Mesh
from jax.sharding import PartitionSpec as P

ITERS = 2
DOM = ("dom_0", "dom_1", "dom_2", "dom_3")


HIGH = lax.Precision.HIGHEST


def with_halo(cells, sides, width):
    for axis, dim in sides:
        count = lax.axis_size(axis)
        ends = count - 1
        head = lax.slice_in_dim(cells, 0, width, axis=dim)
        tail = lax.slice_in_dim(cells, cells.shape[dim] - width, cells.shape[dim], axis=dim)
        cells = jnp.concatenate(
            [
                lax.ppermute(tail, axis, [(i, (i + 1) % count) for i in range(ends)]),
                cells,
                lax.ppermute(head, axis, [((i + 1) % count, i) for i in range(ends)]),
            ],
            axis=dim,
        )
    return cells


def one_axis_at_a_time(array, axes):
    return functools.reduce(lax.psum, axes, array)


def on_device(
    rhs,
    potential,
    precond,
    shift,
    stiffness,
    cell_scale,
    conn,
    cell_count,
    projector,
    support_cell,
    support_atom,
    support_count,
    atom_matrix,
):
    position = lax.axis_index(DOM)
    vectors = rhs.shape[0]
    node_dev = rhs.shape[1]
    slots = conn.shape[0]
    entries = projector.shape[0]
    channels = projector.shape[1]
    owned = atom_matrix.shape[0]
    ghost = node_dev // 16
    live_cells = cell_count[position]
    slot_number = jnp.arange(slots)
    cell_weight = cell_scale * (slot_number < live_cells).astype(jnp.float32)
    entry_live = jnp.arange(entries) < support_count[position]
    support_nodes = conn[support_cell]
    targets = jnp.arange(3 * owned)
    relative = support_atom - (position - 1) * owned
    selector = ((relative[:, None] == targets[None, :]) & entry_live[:, None]).astype(jnp.float32)
    solution = jnp.zeros_like(rhs)
    residual = rhs
    search = precond[None, :] * residual
    smoothed = search
    gamma = jnp.sum(residual * smoothed, axis=1)
    for step in range(ITERS):
        apply_window = with_halo(search, ((DOM, 1),), ghost)
        scaled = apply_window[:, conn] * cell_weight[None, :, None]
        element_out = jnp.einsum("vcn,mn->vcm", scaled, stiffness, precision=HIGH)
        values = apply_window[:, support_nodes]
        partial_value = jnp.einsum("sjn,vsn->jvs", projector, values, precision=HIGH)
        flat = partial_value.reshape(channels * vectors, entries)
        summed = jnp.dot(flat, selector, precision=HIGH).reshape(channels, vectors, -1)
        sides = jnp.concatenate([summed[:, :, :owned], summed[:, :, 2 * owned :]], axis=2)
        arrived = with_halo(sides, ((DOM, 2),), owned)
        mine = summed[:, :, owned : 2 * owned] + arrived[:, :, :owned] + arrived[:, :, 3 * owned :]
        applied = jnp.einsum("aij,jva->iva", atom_matrix, mine, precision=HIGH)
        spread = with_halo(applied, ((DOM, 2),), owned)
        back = jnp.dot(spread.reshape(channels * vectors, -1), selector.T, precision=HIGH)
        back = back.reshape(channels, vectors, entries)
        support_out = jnp.einsum("sjn,jvs->vsn", projector, back, precision=HIGH)
        assembled = jnp.zeros_like(apply_window)
        assembled = assembled.at[:, conn].add(element_out)
        assembled = assembled.at[:, support_nodes].add(support_out)
        rims = jnp.concatenate([assembled[:, :ghost], assembled[:, ghost + node_dev :]], axis=1)
        apply_arrived = with_halo(rims, ((DOM, 1),), ghost)
        inner = assembled[:, ghost : ghost + node_dev]
        inner = inner.at[:, :ghost].add(apply_arrived[:, :ghost])
        inner = inner.at[:, node_dev - ghost :].add(apply_arrived[:, 3 * ghost :])
        image = inner + (potential[None, :] + shift[:, None]) * search
        terms = [jnp.sum(search * image, axis=1)]
        if step == 0:
            terms.append(gamma)
        if step + 1 < ITERS:
            terms.append(jnp.sum(image * smoothed, axis=1))
            terms.append(jnp.sum(image * precond[None, :] * image, axis=1))
        totals = one_axis_at_a_time(jnp.stack(terms), DOM)
        following = 1
        if step == 0:
            gamma = totals[1]
            following = 2
        step_size = gamma / totals[0]
        solution = solution + step_size[:, None] * search
        residual = residual - step_size[:, None] * image
        if step + 1 < ITERS:
            fresh = (
                gamma
                - 2.0 * step_size * totals[following]
                + step_size * step_size * totals[following + 1]
            )
            smoothed = precond[None, :] * residual
            search = smoothed + (fresh / gamma)[:, None] * search
            gamma = fresh
    return (solution, residual)


def solution(mesh):
    torus = Mesh(mesh.devices.reshape(4, 4, 8, 2), ("dom_0", "dom_1", "dom_2", "dom_3"))
    in_specs = (
        P(None, DOM),
        P(DOM),
        P(DOM),
        P(),
        P(),
        P(DOM),
        P(DOM, None),
        P(),
        P(DOM, None, None),
        P(DOM),
        P(DOM),
        P(),
        P(DOM, None, None),
    )
    out_specs = (P(None, DOM), P(None, DOM))
    return jax.shard_map(
        on_device, mesh=torus, in_specs=in_specs, out_specs=out_specs, check_vma=False
    )
```

profile of v0, /device:TPU:1, one launch (start us, length us, event | category | flops | bytes accessed | tf_op | source)
XLA Modules:
  0.0 428.4 jit_solution(9499538204610883644)
XLA Ops:
  0.6 1.0 broadcast_multiply_fusion
  1.7 5.1 %collective-permute-start.1 = (f32[8,416]{1,0:T(8,128)S(1)}, f32[8,416]{1,0:T(8,128)S(1)}, u32[]{:S(2)}, u32[]{:S(2)}) collective-permute-start(f32[8,416]{1,0:T(8,128)S(1)} %get-tuple-element.74), channel_id=1, source_target_pairs={{1,0},{2,1},{3,2},{4,3},{5,4},{6,5},{7,6},{8,7},{9,8},{10,9},{11,1... | collective-permute-start | bytes 39944 | tf_op jit(solution)/shard_map/ppermute | solution.py:26
  6.9 1.9 collective-permute-start
  8.8 0.7 compare_select_fusion.2
  9.5 0.8 compare_select_fusion
  10.3 1.4 gather_fusion.1
  12.0 1.3 dynamic_slice.7
  13.3 0.7 broadcast_subtract_fusion
  13.9 0.6 iota_compare_fusion.1
  14.6 1.3 dynamic_slice.6
  16.0 2.9 copy.107
  18.9 6.9 %gather_fusion.2 = f32[2744,8]{1,0:T(8,128)S(1)} fusion(f32[8,7488]{0,1:T(8,128)} %copy.107, s32[3072]{0:T(1024)S(1)} %pad_clamp_fusion.1), kind=kCustom, calls=%fused_computation.2 | custom fusion | bytes 186592 | tf_op jit(solution)/shard_map/gather | solution.py:77
  27.2 2.2 collective-permute-start.2
  29.4 2.1 collective-permute-start.3
  31.6 0.7 compare_select_fusion.3
  32.2 23.1 %gather_fusion = f32[10976,8]{1,0:T(8,128)} fusion(f32[8,7488]{0,1:T(8,128)} %copy.107, s32[11264]{0:T(1024)S(1)} %pad_clamp_fusion), kind=kCustom, calls=%fused_computation | custom fusion | bytes 746368 | tf_op jit(solution)/shard_map/gather | solution.py:75
  55.3 3.4 copy.108
  59.4 1.9 collective-permute-start.5
  61.3 3.6 collective-permute-start.4
  65.0 1.0 convolution_bitcast_fusion.1
  66.2 3.3 copy.109
  69.5 62.9 %scatter_custom_fusion = f32[8,7488]{0,1:T(8,128)} fusion(s32[10976]{0:T(1024)S(1)} %reshape.234, f32[10976,8]{1,0:T(8,128)} %copy.109, f32[]{:T(128)} %constant.123.clone.1), kind=kCustom, calls=%fused_computation.11 | custom fusion | flops 87808 | bytes 240128 | tf_op jit(solution)/shard_map/scatter-add | solution.py:90
  133.3 0.4 copy.119
  133.7 19.4 %scatter_fusion = f32[8,7488]{0,1:T(8,128)} fusion(f32[8,7488]{0,1:T(8,128)} %scatter_custom_fusion, s32[2744]{0:T(1024)S(1)} %reshape.242, f32[2744,8]{1,0:T(8,128)S(1)} %copy.119), kind=kCustom, calls=%fused_computation.6 | custom fusion | flops 21952 | bytes 274400 | tf_op jit(solution)/shard_map/scatter-add | solution.py:91
  153.1 1.2 fusion.35
  154.4 2.2 collective-permute-start.6
  156.6 0.6 compare_reduce_fusion
  157.2 3.9 slice.177
  161.2 2.4 copy.145
  163.8 2.3 collective-permute-start.7
  166.2 0.7 add_select_fusion.1
  167.2 1.7 collective-permute-done.7
  169.7 18.4 %psum.56 = f32[4,8]{1,0:T(4,128)S(1)} all-reduce(f32[4,8]{1,0:T(4,128)S(1)} %pad_maximum_fusion.2), channel_id=1, replica_groups=mesh['dom_0'=4,'dom_1'=4,'dom_2'=8,'dom_3'=2] {'dom_0'}, use_global_device_ids=true, to_apply=%region_6.0 | all-reduce | flops 32 | bytes 256 | tf_op jit(solution)/shard_map/psum | solution.py:34
  188.1 6.0 %psum.57 = f32[4,8]{1,0:T(4,128)S(1)} all-reduce(f32[4,8]{1,0:T(4,128)S(1)} %psum.56), channel_id=1, replica_groups=mesh['dom_0'=4,'dom_1'=4,'dom_2'=8,'dom_3'=2] {'dom_1'}, use_global_device_ids=true, to_apply=%region_7.0 | all-reduce | flops 32 | bytes 256 | tf_op jit(solution)/shard_map/psum | solution.py:34
  194.1 19.8 %psum.58 = f32[4,8]{1,0:T(4,128)S(1)} all-reduce(f32[4,8]{1,0:T(4,128)S(1)} %psum.57), channel_id=1, replica_groups=mesh['dom_0'=4,'dom_1'=4,'dom_2'=8,'dom_3'=2] {'dom_2'}, use_global_device_ids=true, to_apply=%region_8.0 | all-reduce | flops 32 | bytes 256 | tf_op jit(solution)/shard_map/psum | solution.py:34
  213.8 5.0 %psum.59 = f32[4,8]{1,0:T(4,128)S(1)} all-reduce(f32[4,8]{1,0:T(4,128)S(1)} %psum.58), channel_id=1, replica_groups=mesh['dom_0'=4,'dom_1'=4,'dom_2'=8,'dom_3'=2] {'dom_3'}, use_global_device_ids=true, to_apply=%region_9.0 | all-reduce | flops 32 | bytes 256 | tf_op jit(solution)/shard_map/psum | solution.py:34
  219.1 2.2 collective-permute-start.9
  221.3 3.5 collective-permute-start.8
  224.9 0.8 collective-permute-done.8
  225.9 2.9 copy.124
  228.7 6.9 %gather_fusion.4 = f32[2744,8]{1,0:T(8,128)S(1)} fusion(f32[8,7488]{0,1:T(8,128)} %copy.124, s32[3072]{0:T(1024)S(1)} %pad_clamp_fusion.1), kind=kCustom, calls=%fused_computation.4 | custom fusion | bytes 186592 | tf_op jit(solution)/shard_map/gather | solution.py:77
  237.1 4.2 collective-permute-start.10
  241.3 1.9 collective-permute-start.11
  243.2 23.1 %gather_fusion.3 = f32[10976,8]{1,0:T(8,128)} fusion(f32[8,7488]{0,1:T(8,128)} %copy.124, s32[11264]{0:T(1024)S(1)} %pad_clamp_fusion), kind=kCustom, calls=%fused_computation.3 | custom fusion | bytes 746368 | tf_op jit(solution)/shard_map/gather | solution.py:75
  266.3 3.4 copy.125
  270.3 1.9 collective-permute-start.13
  272.3 3.6 collective-permute-start.12
  275.9 1.0 convolution_bitcast_fusion
  277.2 3.3 copy.126
  280.5 62.9 %scatter_custom_fusion.2 = f32[8,7488]{0,1:T(8,128)} fusion(s32[10976]{0:T(1024)S(1)} %reshape.234, f32[10976,8]{1,0:T(8,128)} %copy.126, f32[]{:T(128)} %constant.123.clone.1), kind=kCustom, calls=%fused_computation.9 | custom fusion | flops 87808 | bytes 240128 | tf_op jit(solution)/shard_map/scatter-add | solution.py:90
  344.2 0.4 copy.136
  344.6 19.4 %scatter_fusion.1 = f32[8,7488]{0,1:T(8,128)} fusion(f32[8,7488]{0,1:T(8,128)} %scatter_custom_fusion.2, s32[2744]{0:T(1024)S(1)} %reshape.242, f32[2744,8]{1,0:T(8,128)S(1)} %copy.136), kind=kCustom, calls=%fused_computation.8 | custom fusion | flops 21952 | bytes 274400 | tf_op jit(solution)/shard_map/scatter-add | solution.py:91
  364.1 1.2 fusion.34
  365.3 2.4 collective-permute-start.14
  367.7 3.9 slice.187
  371.6 2.4 copy.149
  374.3 1.9 collective-permute-start.15
  376.2 0.7 add_select_fusion
  377.2 2.1 collective-permute-done.15
  380.0 16.7 %psum.60 = f32[1,8]{1,0:T(1,128)S(1)} all-reduce(f32[1,8]{1,0:T(1,128)S(1)} %bitcast.102), channel_id=1, replica_groups=mesh['dom_0'=4,'dom_1'=4,'dom_2'=8,'dom_3'=2] {'dom_0'}, use_global_device_ids=true, to_apply=%region_13.0 | all-reduce | flops 8 | bytes 64 | tf_op jit(solution)/shard_map/psum | solution.py:34
  396.7 6.0 %psum.61 = f32[1,8]{1,0:T(1,128)S(1)} all-reduce(f32[1,8]{1,0:T(1,128)S(1)} %psum.60), channel_id=1, replica_groups=mesh['dom_0'=4,'dom_1'=4,'dom_2'=8,'dom_3'=2] {'dom_1'}, use_global_device_ids=true, to_apply=%region_14.0 | all-reduce | flops 8 | bytes 64 | tf_op jit(solution)/shard_map/psum | solution.py:34
  402.7 20.0 %psum.62 = f32[1,8]{1,0:T(1,128)S(1)} all-reduce(f32[1,8]{1,0:T(1,128)S(1)} %psum.61), channel_id=1, replica_groups=mesh['dom_0'=4,'dom_1'=4,'dom_2'=8,'dom_3'=2] {'dom_2'}, use_global_device_ids=true, to_apply=%region_15.0 | all-reduce | flops 8 | bytes 64 | tf_op jit(solution)/shard_map/psum | solution.py:34
  422.8 4.7 %psum.63 = f32[8]{0:T(128)S(1)} all-reduce(f32[8]{0:T(128)S(1)} %bitcast.103), channel_id=1, replica_groups=mesh['dom_0'=4,'dom_1'=4,'dom_2'=8,'dom_3'=2] {'dom_3'}, use_global_device_ids=true, to_apply=%region_16.0 | all-reduce | flops 8 | bytes 64 | tf_op jit(solution)/shard_map/psum | solution.py:34
  427.5 0.9 multiply_subtract_fusion
  (91 shorter events, 9.7 us)
Async XLA Ops:
  0.6 64.3 %copy-start = (f32[343,343]{1,0:T(8,128)S(1)}, f32[343,343]{1,0:T(8,128)}, u32[]{:S(2)}) copy-start(f32[343,343]{1,0:T(8,128)} %param.25) | copy-start | bytes 1411792
  1.7 14.1 %collective-permute-start.1 = (f32[8,416]{1,0:T(8,128)S(1)}, f32[8,416]{1,0:T(8,128)S(1)}, u32[]{:S(2)}, u32[]{:S(2)}) collective-permute-start(f32[8,416]{1,0:T(8,128)S(1)} %get-tuple-element.74), channel_id=1, source_target_pairs={{1,0},{2,1},{3,2},{4,3},{5,4},{6,5},{7,6},{8,7},{9,8},{10,9},{11,1... | collective-permute-start | bytes 39944 | tf_op jit(solution)/shard_map/ppermute | solution.py:26
  6.9 9.0 %collective-permute-start = (f32[8,416]{1,0:T(8,128)S(1)}, f32[8,416]{1,0:T(8,128)S(1)}, u32[]{:S(2)}, u32[]{:S(2)}) collective-permute-start(f32[8,416]{1,0:T(8,128)S(1)} %get-tuple-element.75), channel_id=1, source_target_pairs={{0,1},{1,2},{2,3},{3,4},{4,5},{5,6},{6,7},{7,8},{8,9},{9,10},{10,1... | collective-permute-start | bytes 39944 | tf_op jit(solution)/shard_map/ppermute | solution.py:24
  8.8 17.5 %copy-start.2 = (f32[8,8,343]{2,1,0:T(8,128)S(1)}, f32[8,8,343]{2,1,0:T(8,128)}, u32[]{:S(2)}) copy-start(f32[8,8,343]{2,1,0:T(8,128)} %param.29) | copy-start | bytes 263428
  12.0 19.6 %copy-start.7 = (f32[32]{0:T(128)S(1)}, f32[32]{0:T(128)}, u32[]{:S(2)}) copy-start(f32[32]{0:T(128)} %param.26) | copy-start | bytes 388
  27.2 31.9 %collective-permute-start.2 = (f32[8,8,2]{1,2,0:T(2,128)S(1)}, f32[8,8,2]{1,2,0:T(2,128)S(1)}, u32[]{:S(2)}, u32[]{:S(2)}) collective-permute-start(f32[8,8,2]{1,2,0:T(2,128)S(1)} %get-tuple-element.78), channel_id=1, source_target_pairs={{0,1},{1,2},{2,3},{3,4},{4,5},{5,6},{6,7},{7,8},{8,9},{9,10},{10,1... | collective-permute-start | bytes 1544 | tf_op jit(solution)/shard_map/ppermute | solution.py:24
  29.4 29.7 %collective-permute-start.3 = (f32[8,8,2]{1,2,0:T(2,128)S(1)}, f32[8,8,2]{1,2,0:T(2,128)S(1)}, u32[]{:S(2)}, u32[]{:S(2)}) collective-permute-start(f32[8,8,2]{1,2,0:T(2,128)S(1)} %get-tuple-element.79), channel_id=1, source_target_pairs={{1,0},{2,1},{3,2},{4,3},{5,4},{6,5},{7,6},{8,7},{9,8},{10,9},{11,1... | collective-permute-start | bytes 1544 | tf_op jit(solution)/shard_map/ppermute | solution.py:26
  55.3 3.9 copy-start.5
  59.4 73.0 %collective-permute-start.5 = (f32[8,8,2]{0,1,2:T(8,128)S(1)}, f32[8,8,2]{0,1,2:T(8,128)S(1)}, u32[]{:S(2)}, u32[]{:S(2)}) collective-permute-start(f32[8,8,2]{0,1,2:T(8,128)S(1)} %convolution_bitcast_fusion.7), channel_id=1, source_target_pairs={{1,0},{2,1},{3,2},{4,3},{5,4},{6,5},{7,6},{8,7},{9,8},{10,9},{11,1... | collective-permute-start | bytes 1544 | tf_op jit(solution)/shard_map/ppermute | solution.py:26
  61.3 71.1 %collective-permute-start.4 = (f32[8,8,2]{0,1,2:T(8,128)S(1)}, f32[8,8,2]{0,1,2:T(8,128)S(1)}, u32[]{:S(2)}, u32[]{:S(2)}) collective-permute-start(f32[8,8,2]{0,1,2:T(8,128)S(1)} %convolution_bitcast_fusion.7), channel_id=1, source_target_pairs={{0,1},{1,2},{2,3},{3,4},{4,5},{5,6},{6,7},{7,8},{8,9},{9,10},{10,1... | collective-permute-start | bytes 1544 | tf_op jit(solution)/shard_map/ppermute | solution.py:24
  154.4 11.8 %collective-permute-start.6 = (f32[8,416]{1,0:T(8,128)S(1)}, f32[8,416]{1,0:T(8,128)S(1)}, u32[]{:S(2)}, u32[]{:S(2)}) collective-permute-start(f32[8,416]{1,0:T(8,128)S(1)} %copy.147), channel_id=1, source_target_pairs={{0,1},{1,2},{2,3},{3,4},{4,5},{5,6},{6,7},{7,8},{8,9},{9,10},{10,1... | collective-permute-start | bytes 39944 | tf_op jit(solution)/shard_map/ppermute | solution.py:24
  157.2 12.1 %copy-start.1 = (f32[8,6656]{1,0:T(8,128)S(1)}, f32[8,6656]{1,0:T(8,128)}, u32[]{:S(2)}) copy-start(f32[8,6656]{1,0:T(8,128)} %param.21) | copy-start | bytes 638980
  157.2 12.1 %copy-start.3 = (f32[6656]{0:T(1024)S(1)}, f32[6656]{0:T(1024)}, u32[]{:S(2)}) copy-start(f32[6656]{0:T(1024)} %param.23) | copy-start | bytes 79876
  157.2 12.1 %copy-start.4 = (f32[6656]{0:T(1024)S(1)}, f32[6656]{0:T(1024)}, u32[]{:S(2)}) copy-start(f32[6656]{0:T(1024)} %param.22) | copy-start | bytes 79876
  157.2 12.1 %copy-start.6 = (f32[8]{0:T(128)S(1)}, f32[8]{0:T(128)}, u32[]{:S(2)}) copy-start(f32[8]{0:T(128)} %param.24) | copy-start | bytes 100
  163.8 5.1 %collective-permute-start.7 = (f32[8,416]{1,0:T(8,128)S(1)}, f32[8,416]{1,0:T(8,128)S(1)}, u32[]{:S(2)}, u32[]{:S(2)}) collective-permute-start(f32[8,416]{1,0:T(8,128)S(1)} %copy.148), channel_id=1, source_target_pairs={{1,0},{2,1},{3,2},{4,3},{5,4},{6,5},{7,6},{8,7},{9,8},{10,9},{11,1... | collective-permute-start | bytes 39944 | tf_op jit(solution)/shard_map/ppermute | solution.py:26
  219.1 5.8 %collective-permute-start.9 = (f32[8,416]{1,0:T(8,128)S(1)}, f32[8,416]{1,0:T(8,128)S(1)}, u32[]{:S(2)}, u32[]{:S(2)}) collective-permute-start(f32[8,416]{1,0:T(8,128)S(1)} %get-tuple-element.72), channel_id=1, source_target_pairs={{1,0},{2,1},{3,2},{4,3},{5,4},{6,5},{7,6},{8,7},{9,8},{10,9},{11,1... | collective-permute-start | bytes 39944 | tf_op jit(solution)/shard_map/ppermute | solution.py:26
  221.3 4.4 %collective-permute-start.8 = (f32[8,416]{1,0:T(8,128)S(1)}, f32[8,416]{1,0:T(8,128)S(1)}, u32[]{:S(2)}, u32[]{:S(2)}) collective-permute-start(f32[8,416]{1,0:T(8,128)S(1)} %get-tuple-element.73), channel_id=1, source_target_pairs={{0,1},{1,2},{2,3},{3,4},{4,5},{5,6},{6,7},{7,8},{8,9},{9,10},{10,1... | collective-permute-start | bytes 39944 | tf_op jit(solution)/shard_map/ppermute | solution.py:24
  237.1 33.0 %collective-permute-start.10 = (f32[8,8,2]{1,2,0:T(2,128)S(1)}, f32[8,8,2]{1,2,0:T(2,128)S(1)}, u32[]{:S(2)}, u32[]{:S(2)}) collective-permute-start(f32[8,8,2]{1,2,0:T(2,128)S(1)} %get-tuple-element.76), channel_id=1, source_target_pairs={{0,1},{1,2},{2,3},{3,4},{4,5},{5,6},{6,7},{7,8},{8,9},{9,10},{10,1... | collective-permute-start | bytes 1544 | tf_op jit(solution)/shard_map/ppermute | solution.py:24
  241.3 28.8 %collective-permute-start.11 = (f32[8,8,2]{1,2,0:T(2,128)S(1)}, f32[8,8,2]{1,2,0:T(2,128)S(1)}, u32[]{:S(2)}, u32[]{:S(2)}) collective-permute-start(f32[8,8,2]{1,2,0:T(2,128)S(1)} %get-tuple-element.77), channel_id=1, source_target_pairs={{1,0},{2,1},{3,2},{4,3},{5,4},{6,5},{7,6},{8,7},{9,8},{10,9},{11,1... | collective-permute-start | bytes 1544 | tf_op jit(solution)/shard_map/ppermute | solution.py:26
  270.3 73.0 %collective-permute-start.13 = (f32[8,8,2]{0,1,2:T(8,128)S(1)}, f32[8,8,2]{0,1,2:T(8,128)S(1)}, u32[]{:S(2)}, u32[]{:S(2)}) collective-permute-start(f32[8,8,2]{0,1,2:T(8,128)S(1)} %convolution_bitcast_fusion.6), channel_id=1, source_target_pairs={{1,0},{2,1},{3,2},{4,3},{5,4},{6,5},{7,6},{8,7},{9,8},{10,9},{11,1... | collective-permute-start | bytes 1544 | tf_op jit(solution)/shard_map/ppermute | solution.py:26
  272.3 71.1 %collective-permute-start.12 = (f32[8,8,2]{0,1,2:T(8,128)S(1)}, f32[8,8,2]{0,1,2:T(8,128)S(1)}, u32[]{:S(2)}, u32[]{:S(2)}) collective-permute-start(f32[8,8,2]{0,1,2:T(8,128)S(1)} %convolution_bitcast_fusion.6), channel_id=1, source_target_pairs={{0,1},{1,2},{2,3},{3,4},{4,5},{5,6},{6,7},{7,8},{8,9},{9,10},{10,1... | collective-permute-start | bytes 1544 | tf_op jit(solution)/shard_map/ppermute | solution.py:24
  365.3 10.9 %collective-permute-start.14 = (f32[8,416]{1,0:T(8,128)S(1)}, f32[8,416]{1,0:T(8,128)S(1)}, u32[]{:S(2)}, u32[]{:S(2)}) collective-permute-start(f32[8,416]{1,0:T(8,128)S(1)} %copy.151), channel_id=1, source_target_pairs={{0,1},{1,2},{2,3},{3,4},{4,5},{5,6},{6,7},{7,8},{8,9},{9,10},{10,1... | collective-permute-start | bytes 39944 | tf_op jit(solution)/shard_map/ppermute | solution.py:24
  374.3 5.1 %collective-permute-start.15 = (f32[8,416]{1,0:T(8,128)S(1)}, f32[8,416]{1,0:T(8,128)S(1)}, u32[]{:S(2)}, u32[]{:S(2)}) collective-permute-start(f32[8,416]{1,0:T(8,128)S(1)} %copy.152), channel_id=1, source_target_pairs={{1,0},{2,1},{3,2},{4,3},{5,4},{6,5},{7,6},{8,7},{9,8},{10,9},{11,1... | collective-permute-start | bytes 39944 | tf_op jit(solution)/shard_map/ppermute | solution.py:26
where the time goes:
time: 430 us; the launch traced here: 428 us
  other arithmetic  173 us (40%)
  local copies, waits for them, and re-layouts  105 us (24%)
  blocking collectives  96.6 us (22%)
  starting transfers between devices  43.2 us (10%)
  matrix products  4.8 us (1%)
  waiting for transfers between devices  4.71 us (1%)
    scatter-add x2, other arithmetic, on_device(): assembled = assembled.at[:, conn].add(element_out)  126 us
    psum x8, blocking collectives, one_axis_at_a_time(): return functools.reduce(lax.psum, axes, array)  96.6 us
    gather x6, local copies, waits for them, and re-layouts, on_device(): scaled = apply_window[:, conn] * cell_weight[None, :, None]  53.8 us
    scatter-add x2, other arithmetic, on_device(): assembled = assembled.at[:, support_nodes].add(support_out)  38.9 us
    ppermute x8, starting transfers between devices, with_halo(): lax.ppermute(tail, axis, [(i, (i + 1) % count) for i in range(ends)])  23.7 us
    ppermute x8, starting transfers between devices, with_halo(): lax.ppermute(head, axis, [((i + 1) % count, i) for i in range(ends)])  19.5 us
    gather x6, local copies, waits for them, and re-layouts, on_device(): values = apply_window[:, support_nodes]  14.8 us
  transfers between devices with their start and end apart: 16, of which 3 were waited for; matrix products, arithmetic and copies ran while one was open for 49% of the time, Pallas kernels for 0%

commit v1 on v0

v1 whole, which is shorter than its diff:
```python
import jax
import jax.numpy as jnp
from jax import lax
from jax.experimental import pallas as pl
from jax.experimental.pallas import tpu as pltpu
from jax.sharding import PartitionSpec as P

F32 = jnp.float32
BF16 = jnp.bfloat16
HIGH = lax.Precision.HIGHEST
MESH = pl.DeviceIdType.MESH

VEC = 8
NPROJ = 8
ELEM = 343
PAD = 384
CELLS = 32
PAIRS = CELLS // 2
ENTRIES = 8
OWNED = 2
NODE_DEV = 6656
GHOST = 416
LANES = 256
OWN = NODE_DEV // LANES
EDGE = 2
ROWS = OWN + 2 * EDGE
SHIFT = EDGE * LANES - GHOST
N_DOM = 256


def kernel(
    count_ref,
    support_cell_ref,
    support_atom_ref,
    support_count_ref,
    shift_ref,
    scale_ref,
    rhs_ref,
    pot_ref,
    pre_ref,
    stiff_ref,
    conn_ref,
    proj_ref,
    atom_ref,
    sol_ref,
    res_ref,
    win,
    win_split,
    onehot,
    hi_ref,
    values,
    lhs_hi,
    lhs_lo,
    stiff_hi,
    stiff_lo,
    proj_pad,
    spread_ref,
    product,
    packed,
    acc,
    v_one,
    v_two,
    rim_left,
    rim_right,
    pre_out,
    pre_in,
    atom_in,
    coef_out,
    coef_m2,
    coef_m1,
    coef_p1,
    coef_p2,
    red_out,
    red_in,
    send_sem,
    recv_sem,
):
    me = lax.axis_index("dom")

    def ring(step):
        return lax.rem(me + (step + N_DOM), N_DOM)

    z = lax.rem(lax.div(me, 2), 8)
    x_core = lax.rem(lax.div(me, 16), 4) * 2 + lax.rem(me, 2)
    y = lax.div(me, 64)
    base_z = me - 2 * z
    base_xc = me - 16 * lax.rem(lax.div(me, 16), 4) - lax.rem(me, 2)
    base_y = me - 64 * y

    def z_partner(d):
        return base_z + 2 * lax.rem(z + d, 8)

    def xc_partner(d):
        other = lax.rem(x_core + d, 8)
        return base_xc + 16 * lax.div(other, 2) + lax.rem(other, 2)

    def y_partner(d):
        return base_y + 64 * lax.rem(y + d, 4)

    stages = (
        [z_partner(d) for d in range(1, 8)],
        [xc_partner(d) for d in range(1, 8)],
        [y_partner(d) for d in range(1, 4)],
    )
    greeted = [ring(-2), ring(-1), ring(1), ring(2)]
    for group in stages:
        greeted = greeted + group
    barrier = pltpu.get_barrier_semaphore()
    for other in greeted:
        pl.semaphore_signal(barrier, inc=1, device_id=(other,), device_id_type=MESH)

    used = [0]

    def send(src, dst, target):
        slot = used[0]
        used[0] = slot + 1
        copy = pltpu.make_async_remote_copy(
            src_ref=src,
            dst_ref=dst,
            send_sem=send_sem.at[slot],
            recv_sem=recv_sem.at[slot],
            device_id=(target,),
            device_id_type=MESH,
        )
        copy.start()
        return copy

    def row(ref, index):
        return jnp.broadcast_to(ref[index : index + 1, :], (VEC, 128))

    dot_acc = jnp.zeros((VEC, 128), F32)
    for k in range(OWN):
        for t in range(2):
            column = LANES * k + 128 * t
            r = rhs_ref[:, column : column + 128]
            p = r * row(pre_ref, 2 * k + t)
            win[EDGE + k, :, 128 * t : 128 * t + 128] = p
            dot_acc = dot_acc + r * p
    gamma = jnp.sum(dot_acc, axis=1, keepdims=True)
    pre_out[...] = jnp.zeros_like(pre_out)
    pre_out[0, 0:4, :] = pre_ref[0:4, :]
    pre_out[1, 0:4, :] = pre_ref[48:52, :]

    pl.semaphore_wait(barrier, len(greeted))
    first = [
        send(win.at[EDGE : 2 * EDGE], win.at[ROWS - EDGE : ROWS], ring(-1)),
        send(win.at[OWN : OWN + EDGE], win.at[0:EDGE], ring(1)),
        send(pre_out.at[0], pre_in.at[1], ring(-1)),
        send(pre_out.at[1], pre_in.at[0], ring(1)),
        send(atom_ref, atom_in.at[1], ring(-1)),
        send(atom_ref, atom_in.at[0], ring(1)),
    ]

    position = jnp.full((CELLS, PAD), -1, jnp.int32)
    lane = lax.broadcasted_iota(jnp.int32, (1, PAD), 1)
    spread_ref[...] = position
    spread_ref[:, 0:ELEM] = conn_ref[...] + SHIFT
    for c in range(CELLS):
        hi_ref[c] = spread_ref[c : c + 1, :]

    def build(c, carry):
        number = lax.broadcasted_iota(jnp.int32, (LANES, PAD), 0)
        for q in range(2):
            low = jnp.bitwise_and(hi_ref[2 * c + q], LANES - 1)
            hit = jnp.where(number == low, 1.0, 0.0).astype(BF16)
            onehot[c, :, PAD * q : PAD * q + PAD] = hit
        return carry

    lax.fori_loop(0, PAIRS, build, 0)
    for c in range(CELLS):
        hi_ref[c] = jnp.right_shift(hi_ref[c], 8)
    stiff_hi[...] = jnp.zeros_like(stiff_hi)
    stiff_lo[...] = jnp.zeros_like(stiff_lo)
    stiff = stiff_ref[...]
    top = stiff.astype(BF16)
    stiff_hi[0:ELEM, 0:ELEM] = top
    stiff_lo[0:ELEM, 0:ELEM] = (stiff - top.astype(F32)).astype(BF16)
    proj_pad[...] = jnp.zeros_like(proj_pad)
    proj_pad[:, 0:ELEM] = proj_ref[...]

    lane64 = lax.broadcasted_iota(jnp.int32, (1, 64), 1)
    entry_of = jnp.right_shift(lane64, 3)
    live_entries = support_count_ref[me]
    cell_row = jnp.full((1, 64), -1, jnp.int32)
    atom_row = jnp.full((1, 64), -1, jnp.int32)
    relative = []
    for s in range(ENTRIES):
        live = s < live_entries
        own_atom = jnp.where(live, support_atom_ref[s] - (me - 1) * OWNED, -1)
        relative.append(own_atom)
        cell_row = jnp.where(entry_of == s, support_cell_ref[s], cell_row)
        atom_row = jnp.where(entry_of == s, own_atom, atom_row)
    live_cells = count_ref[me]
    sublane = lax.broadcasted_iota(jnp.int32, (VEC, 128), 0)
    shift_col = jnp.zeros((VEC, 128), F32)
    for v in range(VEC):
        shift_col = jnp.where(sublane == v, shift_ref[v], shift_col)
    r64 = lax.broadcasted_iota(jnp.int32, (64, 48), 0)
    c48 = lax.broadcasted_iota(jnp.int32, (64, 48), 1)
    fold = jnp.where(jnp.bitwise_and(r64, 7) == jnp.bitwise_and(c48, 7), 1.0, 0.0).astype(F32)
    r48 = lax.broadcasted_iota(jnp.int32, (48, 48), 0)
    d48 = lax.broadcasted_iota(jnp.int32, (48, 48), 1)
    same_atom = jnp.right_shift(r48, 3) == jnp.right_shift(d48, 3)
    r8 = lax.broadcasted_iota(jnp.int32, (8, 64), 0)
    c64 = lax.broadcasted_iota(jnp.int32, (8, 64), 1)
    tile8 = jnp.where(r8 == jnp.bitwise_and(c64, 7), 1.0, 0.0).astype(F32)

    for copy in first:
        copy.wait()
    not_first = me > 0
    not_last = me < N_DOM - 1
    for k in range(EDGE):
        win[k] = jnp.where(not_first, win[k], 0.0)
        win[ROWS - EDGE + k] = jnp.where(not_last, win[ROWS - EDGE + k], 0.0)
    atoms = jnp.concatenate([atom_in[0], atom_ref[...], atom_in[1]], axis=0)
    atom_tiled = jnp.dot(atoms, tile8, precision=HIGH, preferred_element_type=F32)

    def gather():
        w = win[...].reshape(ROWS * VEC, LANES)
        wh = w.astype(BF16)
        win_split[:, 0:LANES] = wh
        win_split[:, LANES:] = (w - wh.astype(F32)).astype(BF16)

        def body(c, carry):
            oh = onehot[c]
            g = jnp.dot(win_split[:, 0:LANES], oh, preferred_element_type=F32) + jnp.dot(
                win_split[:, LANES:], oh, preferred_element_type=F32
            )
            his, los = [], []
            for q in range(2):
                cell = 2 * c + q
                weight = jnp.where(cell < live_cells, scale_ref[cell], 0.0)
                parts = []
                for t in range(3):
                    h = jnp.broadcast_to(hi_ref[cell, :, 128 * t : 128 * t + 128], (VEC, 128))
                    got = jnp.zeros((VEC, 128), F32)
                    at = PAD * q + 128 * t
                    for k in range(ROWS):
                        got = jnp.where(h == k, g[VEC * k : VEC * k + VEC, at : at + 128], got)
                    parts.append(got)
                full = jnp.concatenate(parts, axis=1)
                values[cell] = full
                scaled = full * weight
                up = scaled.astype(BF16)
                his.append(up)
                los.append((scaled - up.astype(F32)).astype(BF16))
            lhs_hi[c] = jnp.concatenate(his, axis=0)
            lhs_lo[c] = jnp.concatenate(los, axis=0)
            return carry

        lax.fori_loop(0, PAIRS, body, 0, unroll=2)

    def scatter(first_step, last_step):
        def body(c, carry):
            vs, hs = [], []
            for q in range(2):
                cell = 2 * c + q
                vs.append(packed[cell])
                hs.append(jnp.broadcast_to(hi_ref[cell], (16, PAD)).astype(jnp.int16))
            v = jnp.concatenate(vs, axis=1)
            h = jnp.concatenate(hs, axis=1)
            zero = jnp.zeros_like(v)
            a = jnp.concatenate([jnp.where(h == k, v, zero) for k in range(ROWS)], axis=0)
            acc[...] += lax.dot_general(
                a, onehot[c], (((1,), (1,)), ((), ())), preferred_element_type=F32
            )
            return carry

        lax.fori_loop(first_step, last_step, body, 0, unroll=2)

    def element_work(step):
        picked = jnp.concatenate([values[support_cell_ref[s]] for s in range(ENTRIES)], axis=0)
        cross = lax.dot_general(
            picked,
            proj_pad[...],
            (((1,), (1,)), ((), ())),
            precision=HIGH,
            preferred_element_type=F32,
        )
        own = [jnp.zeros((VEC, 64), F32) for _ in range(3 * OWNED)]
        for s in range(ENTRIES):
            mine = jnp.where(entry_of == s, cross[VEC * s : VEC * s + VEC, :], 0.0)
            for a in range(3 * OWNED):
                own[a] = own[a] + jnp.where(relative[s] == a, mine, 0.0)
        for a in range(3 * OWNED):
            coef_out[step, a, :, 0:64] = own[a]
        coefs = [
            send(coef_out.at[step, 0:4], coef_p1.at[step], ring(-1)),
            send(coef_out.at[step, 2:6], coef_m1.at[step], ring(1)),
            send(coef_out.at[step, 0:2], coef_p2.at[step], ring(-2)),
            send(coef_out.at[step, 4:6], coef_m2.at[step], ring(2)),
        ]
        uh = lhs_hi[...].reshape(CELLS * VEC, PAD)
        ul = lhs_lo[...].reshape(CELLS * VEC, PAD)
        out = jnp.dot(uh, stiff_hi[...], preferred_element_type=F32)
        out = out + jnp.dot(uh, stiff_lo[...], preferred_element_type=F32)
        out = out + jnp.dot(ul, stiff_hi[...], preferred_element_type=F32)
        product[...] = out.reshape(CELLS, VEC, PAD)
        for copy in coefs:
            copy.wait()
        left2, left1 = coef_m2[step], coef_m1[step]
        right1, right2 = coef_p1[step], coef_p2[step]
        total = [
            own[0] + left1[0, :, 0:64] + left2[0, :, 0:64],
            own[1] + left1[1, :, 0:64] + left2[1, :, 0:64],
            own[2] + left1[2, :, 0:64] + right1[0, :, 0:64],
            own[3] + left1[3, :, 0:64] + right1[1, :, 0:64],
            own[4] + right1[2, :, 0:64] + right2[0, :, 0:64],
            own[5] + right1[3, :, 0:64] + right2[1, :, 0:64],
        ]
        stacked = jnp.concatenate(total, axis=0)
        coef = jnp.dot(stacked, fold, precision=HIGH, preferred_element_type=F32)
        coef = jnp.where(same_atom, coef, 0.0)
        term = jnp.dot(coef, atom_tiled, precision=HIGH, preferred_element_type=F32)
        chosen = jnp.zeros((VEC, 64), F32)
        for a in range(3 * OWNED):
            chosen = chosen + jnp.where(atom_row == a, term[VEC * a : VEC * a + VEC, :], 0.0)
        back = jnp.concatenate(
            [jnp.where(cell_row == c, chosen, 0.0) for c in range(CELLS)], axis=0
        )
        support = jnp.dot(back, proj_pad[...], precision=HIGH, preferred_element_type=F32)
        product[...] = product[...] + support.reshape(CELLS, VEC, PAD)

        def pack(c, energy):
            full = product[c]
            up = full.astype(BF16)
            packed[c] = jnp.concatenate([up, (full - up.astype(F32)).astype(BF16)], axis=0)
            return energy + full * values[c]

        return lax.fori_loop(0, CELLS, pack, jnp.zeros((VEC, PAD), F32), unroll=4)

    def diagonal(k, t):
        at = slice(128 * t, 128 * t + 128)
        return (row(pot_ref, 2 * k + t) + shift_col) * win[EDGE + k, :, at]

    gather()
    element_work(0)
    acc[...] = jnp.zeros_like(acc)
    scatter(0, PAIRS)
    for k in range(ROWS):
        both = acc[16 * k : 16 * k + 8, :] + acc[16 * k + 8 : 16 * k + 16, :]
        if EDGE <= k < EDGE + OWN:
            extra = jnp.concatenate([diagonal(k - EDGE, t) for t in range(2)], axis=1)
            both = both + extra
        v_one[k] = both
    rims = [
        send(v_one.at[0 : 2 * EDGE], rim_right.at[0], ring(-1)),
        send(v_one.at[OWN:ROWS], rim_left.at[0], ring(1)),
    ]
    for copy in rims:
        copy.wait()
    for k in range(2 * EDGE):
        v_one[k] = v_one[k] + jnp.where(not_first, rim_left[0, k], 0.0)
        v_one[OWN + k] = v_one[OWN + k] + jnp.where(not_last, rim_right[0, k], 0.0)

    a_acc = jnp.zeros((VEC, 128), F32)
    c_acc = jnp.zeros((VEC, 128), F32)
    d_acc = jnp.zeros((VEC, 128), F32)
    for k in range(OWN):
        for t in range(2):
            at = slice(128 * t, 128 * t + 128)
            image = v_one[EDGE + k, :, at]
            a_acc = a_acc + image * win[EDGE + k, :, at]
            w = image * row(pre_ref, 2 * k + t)
            win[EDGE + k, :, at] = w
            c_acc = c_acc + image * w
            d_acc = d_acc + (row(pot_ref, 2 * k + t) + shift_col) * w * w
    for k in range(EDGE):
        for t in range(2):
            at = slice(128 * t, 128 * t + 128)
            left = row(pre_in.at[0], 2 * k + t) * v_one[k, :, at]
            win[k, :, at] = jnp.where(not_first, left, 0.0)
            right = row(pre_in.at[1], 2 * k + t) * v_one[OWN + EDGE + k, :, at]
            win[OWN + EDGE + k, :, at] = jnp.where(not_last, right, 0.0)

    gather()
    energy = element_work(1)
    for t in range(3):
        d_acc = d_acc + energy[:, 128 * t : 128 * t + 128]
    a_sum = jnp.sum(a_acc, axis=1, keepdims=True)
    c_sum = jnp.sum(c_acc, axis=1, keepdims=True)
    d_sum = jnp.sum(d_acc, axis=1, keepdims=True)
    column = lax.broadcasted_iota(jnp.int32, (VEC, 128), 1)
    tile = jnp.where(
        column == 0,
        gamma,
        jnp.where(column == 1, a_sum, jnp.where(column == 2, c_sum, jnp.where(column == 3, d_sum, 0.0))),
    )

    def reduce_start(stage, value):
        red_out[stage] = value
        at = sum(len(group) for group in stages[:stage])
        return [
            send(red_out.at[stage], red_in.at[at + i], other)
            for i, other in enumerate(stages[stage])
        ]

    def reduce_finish(stage, copies, value):
        for copy in copies:
            copy.wait()
        at = sum(len(group) for group in stages[:stage])
        for i in range(len(copies)):
            value = value + red_in[at + i]
        return value

    acc[...] = jnp.zeros_like(acc)
    going = reduce_start(0, tile)
    scatter(0, 6)
    tile = reduce_finish(0, going, tile)
    going = reduce_start(1, tile)
    scatter(6, 12)
    tile = reduce_finish(1, going, tile)
    going = reduce_start(2, tile)
    scatter(12, PAIRS)
    for k in range(ROWS):
        both = acc[16 * k : 16 * k + 8, :] + acc[16 * k + 8 : 16 * k + 16, :]
        if EDGE <= k < EDGE + OWN:
            extra = jnp.concatenate([diagonal(k - EDGE, t) for t in range(2)], axis=1)
            both = both + extra
        v_two[k] = both
    rims = [
        send(v_two.at[0:EDGE], rim_right.at[1, 0:EDGE], ring(-1)),
        send(v_two.at[ROWS - EDGE : ROWS], rim_left.at[1, 0:EDGE], ring(1)),
    ]
    tile = reduce_finish(2, going, tile)
    scalar = [
        jnp.sum(jnp.where(column == i, tile, 0.0), axis=1, keepdims=True) for i in range(4)
    ]
    gamma, a_sum, c_sum, d_sum = scalar
    step_one = gamma / a_sum
    fresh = gamma - 2.0 * step_one * a_sum + step_one * step_one * c_sum
    grow = 1.0 + fresh / gamma
    curve = grow * grow * a_sum - 2.0 * grow * step_one * c_sum + step_one * step_one * d_sum
    step_two = fresh / curve
    along = jnp.broadcast_to(step_one + step_two * grow, (VEC, 128))
    across = jnp.broadcast_to(step_one * step_two, (VEC, 128))
    for copy in rims:
        copy.wait()
    for k in range(EDGE):
        v_two[EDGE + k] = v_two[EDGE + k] + jnp.where(not_first, rim_left[1, k], 0.0)
        v_two[OWN + k] = v_two[OWN + k] + jnp.where(not_last, rim_right[1, k], 0.0)
    for k in range(OWN):
        for t in range(2):
            at = slice(128 * t, 128 * t + 128)
            col = slice(LANES * k + 128 * t, LANES * k + 128 * t + 128)
            r = rhs_ref[:, col]
            p = r * row(pre_ref, 2 * k + t)
            sol_ref[:, col] = along * p - across * win[EDGE + k, :, at]
            res_ref[:, col] = r - along * v_one[EDGE + k, :, at] + across * v_two[EDGE + k, :, at]


SENDS = 6 + 2 * 4 + 2 * 2 + 17


def on_device(
    rhs,
    potential,
    precond,
    shift,
    stiffness,
    cell_scale,
    conn,
    cell_count,
    projector,
    support_cell,
    support_atom,
    support_count,
    atom_matrix,
):
    vmem = pl.BlockSpec(memory_space=pltpu.VMEM)
    smem = pl.BlockSpec(memory_space=pltpu.SMEM)
    shape = jax.ShapeDtypeStruct((VEC, NODE_DEV), F32)
    return pl.pallas_call(
        kernel,
        name="pcg",
        out_shape=(shape, shape),
        in_specs=[smem] * 6 + [vmem] * 7,
        out_specs=(vmem, vmem),
        scratch_shapes=[
            pltpu.VMEM((ROWS, VEC, LANES), F32),
            pltpu.VMEM((ROWS * VEC, 2 * LANES), BF16),
            pltpu.VMEM((PAIRS, LANES, 2 * PAD), BF16),
            pltpu.VMEM((CELLS, 1, PAD), jnp.int32),
            pltpu.VMEM((CELLS, VEC, PAD), F32),
            pltpu.VMEM((PAIRS, 16, PAD), BF16),
            pltpu.VMEM((PAIRS, 16, PAD), BF16),
            pltpu.VMEM((PAD, PAD), BF16),
            pltpu.VMEM((PAD, PAD), BF16),
            pltpu.VMEM((ENTRIES * NPROJ, PAD), F32),
            pltpu.VMEM((CELLS, PAD), jnp.int32),
            pltpu.VMEM((CELLS, VEC, PAD), F32),
            pltpu.VMEM((CELLS, 16, PAD), BF16),
            pltpu.VMEM((ROWS * 16, LANES), F32),
            pltpu.VMEM((ROWS, VEC, LANES), F32),
            pltpu.VMEM((ROWS, VEC, LANES), F32),
            pltpu.VMEM((2, 2 * EDGE, VEC, LANES), F32),
            pltpu.VMEM((2, 2 * EDGE, VEC, LANES), F32),
            pltpu.VMEM((2, 8, 128), F32),
            pltpu.VMEM((2, 8, 128), F32),
            pltpu.VMEM((2, OWNED * NPROJ, NPROJ), F32),
            pltpu.VMEM((2, 3 * OWNED, VEC, 128), F32),
            pltpu.VMEM((2, 2, VEC, 128), F32),
            pltpu.VMEM((2, 4, VEC, 128), F32),
            pltpu.VMEM((2, 4, VEC, 128), F32),
            pltpu.VMEM((2, 2, VEC, 128), F32),
            pltpu.VMEM((3, VEC, 128), F32),
            pltpu.VMEM((17, VEC, 128), F32),
            pltpu.SemaphoreType.DMA((SENDS,)),
            pltpu.SemaphoreType.DMA((SENDS,)),
        ],
        compiler_params=pltpu.CompilerParams(
            collective_id=0, has_side_effects=True, vmem_limit_bytes=40 << 20
        ),
    )(
        cell_count,
        support_cell,
        support_atom,
        support_count,
        shift,
        cell_scale,
        rhs,
        potential.reshape(52, 128),
        precond.reshape(52, 128),
        stiffness,
        conn,
        projector.reshape(ENTRIES * NPROJ, ELEM),
        atom_matrix.reshape(OWNED * NPROJ, NPROJ),
    )


def solution(mesh):
    in_specs = (
        P(None, "dom"),
        P("dom"),
        P("dom"),
        P(),
        P(),
        P("dom"),
        P("dom", None),
        P(),
        P("dom", None, None),
        P("dom"),
        P("dom"),
        P(),
        P("dom", None, None),
    )
    out_specs = (P(None, "dom"), P(None, "dom"))
    return jax.shard_map(
        on_device, mesh=mesh, in_specs=in_specs, out_specs=out_specs, check_vma=False
    )
```

time: 430 us -> 69.4 us (0.16)
  the two profiles are of different devices: /device:TPU:1 before, /device:TPU:8 now
where the time goes in v1:
time: 69.4 us; the launch traced here: 68.9 us
  Pallas kernels  60.3 us (87%)
  local copies, waits for them, and re-layouts  7.92 us (11%)
  between operations  0.7 us (1%)
    pallas_call x1, Pallas kernels, on_device(): pl.pallas_call(kernel, name='pcg', out_shape=(shape, shape), in_specs=[sm...  60.3 us
    unnamed x28, local copies, waits for them, and re-layouts  7.92 us

profile of v1, /device:TPU:8, one launch (start us, length us, event | category | flops | bytes accessed | tf_op | source)
XLA Modules:
  0.0 68.9 jit_solution(10982578833190646565)
XLA Ops:
  0.6 0.0 copy-start.12
  0.6 0.0 copy-start.8
  0.7 0.0 copy-start.10
  0.7 0.0 copy-start.11
  0.7 0.0 copy-start.7
  0.7 0.0 copy-start.9
  0.7 0.6 copy-done.12
  1.3 0.0 copy-done.8
  1.3 0.0 copy-done.10
  1.3 0.0 copy-done.11
  1.3 0.0 copy-done.7
  1.4 0.0 copy-done.9
  1.4 0.0 copy-start
  1.4 1.0 %copy-done = f32[343,343]{1,0:T(8,128)S(1)} copy-done((f32[343,343]{1,0:T(8,128)S(1)}, f32[343,343]{1,0:T(8,128)}, u32[]{:S(2)}) %copy-start) | copy-done | bytes 470620
  2.4 0.0 copy-start.1
  2.4 0.9 %copy-done.1 = f32[8,6656]{1,0:T(8,128)S(1)} copy-done((f32[8,6656]{1,0:T(8,128)S(1)}, f32[8,6656]{1,0:T(8,128)}, u32[]{:S(2)}) %copy-start.1) | copy-done | bytes 213016
  3.4 0.0 copy-start.2
  3.4 0.9 %copy-done.2 = f32[8,8,343]{2,1,0:T(8,128)S(1)} copy-done((f32[8,8,343]{2,1,0:T(8,128)S(1)}, f32[8,8,343]{2,1,0:T(8,128)}, u32[]{:S(2)}) %copy-start.2) | copy-done | bytes 87832
  4.3 0.0 copy-start.3
  4.3 0.8 %copy-done.3 = s32[32,343]{1,0:T(8,128)S(1)} copy-done((s32[32,343]{1,0:T(8,128)S(1)}, s32[32,343]{1,0:T(8,128)}, u32[]{:S(2)}) %copy-start.3) | copy-done | bytes 43928
  5.1 0.0 copy-start.4
  5.1 0.7 %copy-done.4 = f32[6656]{0:T(1024)S(1)} copy-done((f32[6656]{0:T(1024)S(1)}, f32[6656]{0:T(1024)}, u32[]{:S(2)}) %copy-start.4) | copy-done | bytes 26648
  5.8 0.0 copy-start.5
  5.8 0.7 %copy-done.5 = f32[6656]{0:T(1024)S(1)} copy-done((f32[6656]{0:T(1024)S(1)}, f32[6656]{0:T(1024)}, u32[]{:S(2)}) %copy-start.5) | copy-done | bytes 26648
  6.5 0.0 copy-start.6
  6.5 0.7 %copy-done.6 = f32[2,8,8]{2,1,0:T(8,128)S(1)} copy-done((f32[2,8,8]{2,1,0:T(8,128)S(1)}, f32[2,8,8]{2,1,0:T(8,128)}, u32[]{:S(2)}) %copy-start.6) | copy-done | bytes 536
  7.2 60.3 %pcg.1 = (f32[8,6656]{1,0:T(8,128)S(1)}, f32[8,6656]{1,0:T(8,128)S(1)}) custom-call(s32[256]{0:T(256)S(1)} %copy-done.7, s32[8]{0:T(128)S(1)} %copy-done.9, s32[8]{0:T(128)S(1)} %copy-done.10, s32[256]{0:T(256)S(1)} %copy-done.8, f32[8]{0:T(128)S(1)} %copy-done.11, f32[32]{0:T(128)S(1)} %copy-done.12, f32[8,6656]{1,0:T(8,128)S(1)} %copy-done.1, ...), custom_call_target="tpu_custom_call" | custom-call | tf_op jit(solution)/shard_map/pcg/pallas_call | solution.py:473
  67.6 0.7 copy.20
  68.3 0.7 copy.21
Async XLA Ops:
  0.6 0.7 copy-start.12
  0.6 0.7 copy-start.8
  0.7 0.7 copy-start.10
  0.7 0.7 copy-start.11
  0.7 0.7 %copy-start.7 = (s32[256]{0:T(256)S(1)}, s32[256]{0:T(256)}, u32[]{:S(2)}) copy-start(s32[256]{0:T(256)} %count_ref.1) | copy-start | bytes 3076
  0.7 0.7 %copy-start.9 = (s32[8]{0:T(128)S(1)}, s32[8]{0:T(128)}, u32[]{:S(2)}) copy-start(s32[8]{0:T(128)} %support_cell_ref.1) | copy-start | bytes 100
  1.4 1.0 %copy-start = (f32[343,343]{1,0:T(8,128)S(1)}, f32[343,343]{1,0:T(8,128)}, u32[]{:S(2)}) copy-start(f32[343,343]{1,0:T(8,128)} %stiff_ref.1) | copy-start | bytes 1411792
  2.4 0.9 %copy-start.1 = (f32[8,6656]{1,0:T(8,128)S(1)}, f32[8,6656]{1,0:T(8,128)}, u32[]{:S(2)}) copy-start(f32[8,6656]{1,0:T(8,128)} %rhs_ref.1) | copy-start | bytes 638980
  3.4 0.9 %copy-start.2 = (f32[8,8,343]{2,1,0:T(8,128)S(1)}, f32[8,8,343]{2,1,0:T(8,128)}, u32[]{:S(2)}) copy-start(f32[8,8,343]{2,1,0:T(8,128)} %param.21) | copy-start | bytes 263428
  4.3 0.8 %copy-start.3 = (s32[32,343]{1,0:T(8,128)S(1)}, s32[32,343]{1,0:T(8,128)}, u32[]{:S(2)}) copy-start(s32[32,343]{1,0:T(8,128)} %conn_ref.1) | copy-start | bytes 131716
  5.1 0.7 %copy-start.4 = (f32[6656]{0:T(1024)S(1)}, f32[6656]{0:T(1024)}, u32[]{:S(2)}) copy-start(f32[6656]{0:T(1024)} %param.14) | copy-start | bytes 79876
  5.8 0.7 %copy-start.5 = (f32[6656]{0:T(1024)S(1)}, f32[6656]{0:T(1024)}, u32[]{:S(2)}) copy-start(f32[6656]{0:T(1024)} %param.15) | copy-start | bytes 79876
  6.5 0.7 %copy-start.6 = (f32[2,8,8]{2,1,0:T(8,128)S(1)}, f32[2,8,8]{2,1,0:T(8,128)}, u32[]{:S(2)}) copy-start(f32[2,8,8]{2,1,0:T(8,128)} %param.25) | copy-start | bytes 1540

commit v2 on v1

v2 whole, which is shorter than its diff:
```python
import jax
import jax.numpy as jnp
from jax import lax
from jax.experimental import pallas as pl
from jax.experimental.pallas import tpu as pltpu
from jax.sharding import PartitionSpec as P

F32 = jnp.float32
BF16 = jnp.bfloat16
HIGH = lax.Precision.HIGHEST
MESH = pl.DeviceIdType.MESH

VEC = 8
NPROJ = 8
ELEM = 343
PAD = 384
CELLS = 32
PAIRS = CELLS // 2
ENTRIES = 8
SLOTS = CELLS + ENTRIES
SLOT_PAIRS = SLOTS // 2
OWNED = 2
NODE_DEV = 6656
GHOST = 416
LANES = 256
OWN = NODE_DEV // LANES
EDGE = 2
ROWS = OWN + 2 * EDGE
SHIFT = EDGE * LANES - GHOST
N_DOM = 256


def kernel(
    count_ref,
    support_cell_ref,
    support_atom_ref,
    support_count_ref,
    shift_ref,
    scale_ref,
    rhs_hbm,
    pot_hbm,
    pre_hbm,
    stiff_hbm,
    conn_hbm,
    proj_hbm,
    atom_hbm,
    sol_ref,
    res_ref,
    rhs_ref,
    pot_ref,
    pre_ref,
    stiff_ref,
    conn_ref,
    proj_ref,
    atom_ref,
    win,
    split_main,
    split_rim,
    onehot,
    pos_ref,
    hi_ref,
    hi_wide,
    values,
    lhs_hi,
    lhs_lo,
    stiff_hi,
    stiff_lo,
    proj_pad,
    spread_ref,
    packed,
    acc,
    v_one,
    v_two,
    rim_left,
    rim_right,
    pre_out,
    pre_in,
    atom_in,
    coef_out,
    coef_m2,
    coef_m1,
    coef_p1,
    coef_p2,
    red_out,
    red_in,
    load_sem,
    send_sem,
    recv_sem,
):
    me = lax.axis_index("dom")

    def ring(step):
        return lax.rem(me + (step + N_DOM), N_DOM)

    low16 = lax.rem(me, 16)
    high16 = lax.div(me, 16)
    stages = (
        [me - low16 + lax.rem(low16 + d, 16) for d in range(1, 16)],
        [low16 + 16 * lax.rem(high16 + d, 16) for d in range(1, 16)],
    )
    greeted = [ring(-2), ring(-1), ring(1), ring(2)]
    for group in stages:
        greeted = greeted + group
    barrier = pltpu.get_barrier_semaphore()
    for other in greeted:
        pl.semaphore_signal(barrier, inc=1, device_id=(other,), device_id_type=MESH)

    loads = []
    for i, (src, dst) in enumerate(
        (
            (conn_hbm, conn_ref),
            (rhs_hbm, rhs_ref),
            (pre_hbm, pre_ref),
            (atom_hbm, atom_ref),
            (proj_hbm, proj_ref),
            (stiff_hbm, stiff_ref),
            (pot_hbm, pot_ref),
        )
    ):
        load = pltpu.make_async_copy(src, dst, load_sem.at[i])
        load.start()
        loads.append(load)

    used = [0]

    def send(src, dst, target):
        slot = used[0]
        used[0] = slot + 1
        copy = pltpu.make_async_remote_copy(
            src_ref=src,
            dst_ref=dst,
            send_sem=send_sem.at[slot],
            recv_sem=recv_sem.at[slot],
            device_id=(target,),
            device_id_type=MESH,
        )
        copy.start()
        return copy

    def row(ref, index):
        return jnp.broadcast_to(ref[index : index + 1, :], (VEC, 128))

    for load in loads[1:4]:
        load.wait()
    dot_acc = jnp.zeros((VEC, 128), F32)
    for k in range(OWN):
        for t in range(2):
            column = LANES * k + 128 * t
            r = rhs_ref[:, column : column + 128]
            p = r * row(pre_ref, 2 * k + t)
            win[EDGE + k, :, 128 * t : 128 * t + 128] = p
            dot_acc = dot_acc + r * p
    gamma = jnp.sum(dot_acc, axis=1, keepdims=True)
    pre_out[...] = jnp.zeros_like(pre_out)
    pre_out[0, 0:4, :] = pre_ref[0:4, :]
    pre_out[1, 0:4, :] = pre_ref[48:52, :]
    pl.semaphore_wait(barrier, len(greeted))
    first = [
        send(win.at[EDGE : 2 * EDGE], win.at[ROWS - EDGE : ROWS], ring(-1)),
        send(win.at[OWN : OWN + EDGE], win.at[0:EDGE], ring(1)),
        send(pre_out.at[0], pre_in.at[1], ring(-1)),
        send(pre_out.at[1], pre_in.at[0], ring(1)),
        send(atom_ref, atom_in.at[1], ring(-1)),
        send(atom_ref, atom_in.at[0], ring(1)),
    ]

    loads[0].wait()
    spread_ref[...] = jnp.full((CELLS, PAD), -1, jnp.int32)
    spread_ref[:, 0:ELEM] = conn_ref[...] + SHIFT
    for c in range(CELLS):
        pos_ref[c] = spread_ref[c : c + 1, :]
    for s in range(ENTRIES):
        pos_ref[CELLS + s] = pos_ref[support_cell_ref[s]]
    number = lax.broadcasted_iota(jnp.int32, (LANES, PAD), 0).astype(jnp.int16)

    def build(c, carry):
        for q in range(2):
            slot = 2 * c + q
            place = pos_ref[slot]
            high = jnp.right_shift(place, 8)
            hi_ref[slot] = high
            hi_wide[slot] = jnp.broadcast_to(high, (16, PAD)).astype(jnp.int16)
            low = jnp.bitwise_and(place, LANES - 1)
            low = jnp.broadcast_to(low, (16, PAD)).astype(jnp.int16)
            one = jnp.ones((16, PAD), BF16)
            zero = jnp.zeros((16, PAD), BF16)
            for r in range(LANES // 16):
                hit = jnp.where(number[16 * r : 16 * r + 16, :] == low, one, zero)
                onehot[c, 16 * r : 16 * r + 16, PAD * q : PAD * q + PAD] = hit
        return carry

    lax.fori_loop(0, SLOT_PAIRS, build, 0)

    live_cells = count_ref[me]

    def split(block):
        up = block.astype(BF16)
        return up, (block - up.astype(F32)).astype(BF16)

    def gather_main(blocks):
        count = len(blocks) * VEC
        for i, k in enumerate(blocks):
            up, down = split(win[k])
            split_main[0, VEC * i : VEC * i + VEC, :] = up
            split_main[1, VEC * i : VEC * i + VEC, :] = down

        def body(c, carry):
            oh = onehot[c]
            g = jnp.dot(split_main[0, 0:count, :], oh, preferred_element_type=F32) + jnp.dot(
                split_main[1, 0:count, :], oh, preferred_element_type=F32
            )
            for q in range(2):
                for t in range(3):
                    h = jnp.broadcast_to(
                        hi_ref[2 * c + q, :, 128 * t : 128 * t + 128], (VEC, 128)
                    )
                    got = jnp.zeros((VEC, 128), F32)
                    at = PAD * q + 128 * t
                    for i, k in enumerate(blocks):
                        got = jnp.where(h == k, g[VEC * i : VEC * i + VEC, at : at + 128], got)
                    values[2 * c + q, :, 128 * t : 128 * t + 128] = got
            return carry

        lax.fori_loop(0, SLOT_PAIRS, body, 0, unroll=4)

    def prepare_rim(blocks):
        count = len(blocks) * VEC
        for i, k in enumerate(blocks):
            up, down = split(win[k])
            split_rim[VEC * i : VEC * i + VEC, :] = up
            split_rim[count + VEC * i : count + VEC * i + VEC, :] = down

    def gather_rim(blocks, first_pair, last_pair, cells):
        count = len(blocks) * VEC

        def body(c, carry):
            g = jnp.dot(split_rim[0 : 2 * count, :], onehot[c], preferred_element_type=F32)
            g = g[0:count] + g[count : 2 * count]
            ups, downs = [], []
            for q in range(2):
                slot = 2 * c + q
                parts = []
                for t in range(3):
                    h = jnp.broadcast_to(hi_ref[slot, :, 128 * t : 128 * t + 128], (VEC, 128))
                    got = values[slot, :, 128 * t : 128 * t + 128]
                    at = PAD * q + 128 * t
                    for i, k in enumerate(blocks):
                        got = jnp.where(h == k, g[VEC * i : VEC * i + VEC, at : at + 128], got)
                    parts.append(got)
                full = jnp.concatenate(parts, axis=1)
                values[slot] = full
                if cells:
                    weight = jnp.where(slot < live_cells, scale_ref[slot], 0.0)
                    up, down = split(full * weight)
                    ups.append(up)
                    downs.append(down)
            if cells:
                lhs_hi[c] = jnp.concatenate(ups, axis=0)
                lhs_lo[c] = jnp.concatenate(downs, axis=0)
            return carry

        lax.fori_loop(first_pair, last_pair, body, 0, unroll=4)

    def scatter(first_pair, last_pair):
        def body(c, carry):
            v = jnp.concatenate([packed[2 * c], packed[2 * c + 1]], axis=1)
            h = jnp.concatenate([hi_wide[2 * c], hi_wide[2 * c + 1]], axis=1)
            zero = jnp.zeros_like(v)
            a = jnp.concatenate([jnp.where(h == k, v, zero) for k in range(ROWS)], axis=0)
            acc[...] += lax.dot_general(
                a, onehot[c], (((1,), (1,)), ((), ())), preferred_element_type=F32
            )
            return carry

        lax.fori_loop(first_pair, last_pair, body, 0, unroll=4)

    own_blocks = list(range(EDGE, EDGE + OWN))
    ghost_blocks = list(range(EDGE)) + list(range(EDGE + OWN, ROWS))
    inner_blocks = list(range(2 * EDGE, OWN))
    rim_blocks = list(range(2 * EDGE)) + list(range(OWN, ROWS))

    gather_main(own_blocks)

    for load in loads[4:]:
        load.wait()
    stiff_hi[...] = jnp.zeros_like(stiff_hi)
    stiff_lo[...] = jnp.zeros_like(stiff_lo)
    up, down = split(stiff_ref[...])
    stiff_hi[0:ELEM, 0:ELEM] = up
    stiff_lo[0:ELEM, 0:ELEM] = down
    proj_pad[...] = jnp.zeros_like(proj_pad)
    proj_pad[:, 0:ELEM] = proj_ref[...]

    lane64 = lax.broadcasted_iota(jnp.int32, (1, 64), 1)
    entry_of = jnp.right_shift(lane64, 3)
    live_entries = support_count_ref[me]
    atom_row = jnp.full((1, 64), -1, jnp.int32)
    relative = []
    for s in range(ENTRIES):
        own_atom = jnp.where(s < live_entries, support_atom_ref[s] - (me - 1) * OWNED, -1)
        relative.append(own_atom)
        atom_row = jnp.where(entry_of == s, own_atom, atom_row)
    sublane = lax.broadcasted_iota(jnp.int32, (VEC, 128), 0)
    shift_col = jnp.zeros((VEC, 128), F32)
    for v in range(VEC):
        shift_col = jnp.where(sublane == v, shift_ref[v], shift_col)
    r64 = lax.broadcasted_iota(jnp.int32, (64, 48), 0)
    c48 = lax.broadcasted_iota(jnp.int32, (64, 48), 1)
    fold = jnp.where(jnp.bitwise_and(r64, 7) == jnp.bitwise_and(c48, 7), 1.0, 0.0).astype(F32)
    r48 = lax.broadcasted_iota(jnp.int32, (48, 48), 0)
    d48 = lax.broadcasted_iota(jnp.int32, (48, 48), 1)
    same_atom = jnp.right_shift(r48, 3) == jnp.right_shift(d48, 3)
    r8 = lax.broadcasted_iota(jnp.int32, (8, 64), 0)
    c64 = lax.broadcasted_iota(jnp.int32, (8, 64), 1)
    tile8 = jnp.where(r8 == jnp.bitwise_and(c64, 7), 1.0, 0.0).astype(F32)
    for copy in first:
        copy.wait()
    not_first = me > 0
    not_last = me < N_DOM - 1
    for k in range(EDGE):
        win[k] = jnp.where(not_first, win[k], 0.0)
        win[ROWS - EDGE + k] = jnp.where(not_last, win[ROWS - EDGE + k], 0.0)
    atoms = jnp.concatenate([atom_in[0], atom_ref[...], atom_in[1]], axis=0)
    atom_tiled = jnp.dot(atoms, tile8, precision=HIGH, preferred_element_type=F32)

    def coef_start(step):
        picked = values[CELLS:SLOTS].reshape(ENTRIES * VEC, PAD)
        cross = lax.dot_general(
            picked,
            proj_pad[...],
            (((1,), (1,)), ((), ())),
            precision=HIGH,
            preferred_element_type=F32,
        )
        own = [jnp.zeros((VEC, 64), F32) for _ in range(3 * OWNED)]
        for s in range(ENTRIES):
            mine = jnp.where(entry_of == s, cross[VEC * s : VEC * s + VEC, :], 0.0)
            for a in range(3 * OWNED):
                own[a] = own[a] + jnp.where(relative[s] == a, mine, 0.0)
        for a in range(3 * OWNED):
            coef_out[step, a, :, 0:64] = own[a]
        copies = [
            send(coef_out.at[step, 0:4], coef_p1.at[step], ring(-1)),
            send(coef_out.at[step, 2:6], coef_m1.at[step], ring(1)),
            send(coef_out.at[step, 0:2], coef_p2.at[step], ring(-2)),
            send(coef_out.at[step, 4:6], coef_m2.at[step], ring(2)),
        ]
        return copies

    def coef_finish(step, copies):
        for copy in copies:
            copy.wait()
        own = coef_out[step, :, :, 0:64]
        left2, left1 = coef_m2[step, :, :, 0:64], coef_m1[step, :, :, 0:64]
        right1, right2 = coef_p1[step, :, :, 0:64], coef_p2[step, :, :, 0:64]
        total = [
            own[0] + left1[0] + left2[0],
            own[1] + left1[1] + left2[1],
            own[2] + left1[2] + right1[0],
            own[3] + left1[3] + right1[1],
            own[4] + right1[2] + right2[0],
            own[5] + right1[3] + right2[1],
        ]
        stacked = jnp.concatenate(total, axis=0)
        coef = jnp.dot(stacked, fold, precision=HIGH, preferred_element_type=F32)
        coef = jnp.where(same_atom, coef, 0.0)
        term = jnp.dot(coef, atom_tiled, precision=HIGH, preferred_element_type=F32)
        both = coef[2 * VEC : 4 * VEC, :] * term[2 * VEC : 4 * VEC, 0:48]
        energy = jnp.sum(both[0:VEC] + both[VEC : 2 * VEC], axis=1, keepdims=True)
        return term, energy

    def support_products(term):
        chosen = jnp.zeros((VEC, 64), F32)
        for a in range(3 * OWNED):
            chosen = chosen + jnp.where(atom_row == a, term[VEC * a : VEC * a + VEC, :], 0.0)
        back = jnp.concatenate(
            [jnp.where(entry_of == s, chosen, 0.0) for s in range(ENTRIES)], axis=0
        )
        out = jnp.dot(back, proj_pad[...], precision=HIGH, preferred_element_type=F32)
        for s in range(ENTRIES):
            up, down = split(out[VEC * s : VEC * s + VEC, :])
            packed[CELLS + s] = jnp.concatenate([up, down], axis=0)

    def cell_products():
        uh = lhs_hi[...].reshape(CELLS * VEC, PAD)
        ul = lhs_lo[...].reshape(CELLS * VEC, PAD)
        out = jnp.dot(uh, stiff_hi[...], preferred_element_type=F32)
        out = out + jnp.dot(uh, stiff_lo[...], preferred_element_type=F32)
        out = out + jnp.dot(ul, stiff_hi[...], preferred_element_type=F32)
        energy = jnp.zeros((VEC, PAD), F32)
        for c in range(CELLS):
            full = out[VEC * c : VEC * c + VEC, :]
            up, down = split(full)
            packed[c] = jnp.concatenate([up, down], axis=0)
            energy = energy + full * values[c]
        return energy

    def assembled(k):
        both = acc[16 * k : 16 * k + 8, :] + acc[16 * k + 8 : 16 * k + 16, :]
        if EDGE <= k < EDGE + OWN:
            extra = []
            for t in range(2):
                diagonal = row(pot_ref, 2 * (k - EDGE) + t) + shift_col
                extra.append(diagonal * win[k, :, 128 * t : 128 * t + 128])
            both = both + jnp.concatenate(extra, axis=1)
        return both

    prepare_rim(ghost_blocks)
    gather_rim(ghost_blocks, PAIRS, SLOT_PAIRS, False)
    coefs = coef_start(0)
    gather_rim(ghost_blocks, 0, PAIRS, True)
    cell_products()
    acc[...] = jnp.zeros_like(acc)
    scatter(0, PAIRS)
    term, _ = coef_finish(0, coefs)
    support_products(term)
    scatter(PAIRS, SLOT_PAIRS)
    for k in rim_blocks:
        v_one[k] = assembled(k)
    rims = [
        send(v_one.at[0 : 2 * EDGE], rim_right.at[0], ring(-1)),
        send(v_one.at[OWN:ROWS], rim_left.at[0], ring(1)),
    ]
    for k in inner_blocks:
        v_one[k] = assembled(k)

    sums = [jnp.zeros((VEC, 128), F32) for _ in range(3)]

    def advance(k, sums):
        a_acc, c_acc, d_acc = sums
        for t in range(2):
            at = slice(128 * t, 128 * t + 128)
            index = 2 * (k - EDGE) + t
            image = v_one[k, :, at]
            a_acc = a_acc + image * win[k, :, at]
            w = image * row(pre_ref, index)
            win[k, :, at] = w
            c_acc = c_acc + image * w
            d_acc = d_acc + (row(pot_ref, index) + shift_col) * w * w
        return [a_acc, c_acc, d_acc]

    for k in inner_blocks:
        sums = advance(k, sums)
    gather_main(inner_blocks)
    for copy in rims:
        copy.wait()
    for k in range(2 * EDGE):
        v_one[k] = v_one[k] + jnp.where(not_first, rim_left[0, k], 0.0)
        v_one[OWN + k] = v_one[OWN + k] + jnp.where(not_last, rim_right[0, k], 0.0)
    for k in rim_blocks:
        if EDGE <= k < EDGE + OWN:
            sums = advance(k, sums)
    for k in range(EDGE):
        for t in range(2):
            at = slice(128 * t, 128 * t + 128)
            left = row(pre_in.at[0], 2 * k + t) * v_one[k, :, at]
            win[k, :, at] = jnp.where(not_first, left, 0.0)
            right = row(pre_in.at[1], 2 * k + t) * v_one[OWN + EDGE + k, :, at]
            win[OWN + EDGE + k, :, at] = jnp.where(not_last, right, 0.0)

    prepare_rim(rim_blocks)
    gather_rim(rim_blocks, PAIRS, SLOT_PAIRS, False)
    coefs = coef_start(1)
    gather_rim(rim_blocks, 0, PAIRS, True)
    energy = cell_products()
    acc[...] = jnp.zeros_like(acc)
    scatter(0, 12)
    term, support_energy = coef_finish(1, coefs)

    a_acc, c_acc, d_acc = sums
    for t in range(3):
        d_acc = d_acc + energy[:, 128 * t : 128 * t + 128]
    column = lax.broadcasted_iota(jnp.int32, (VEC, 128), 1)
    tile = jnp.zeros((VEC, 128), F32)
    locals_ = (
        gamma,
        jnp.sum(a_acc, axis=1, keepdims=True),
        jnp.sum(c_acc, axis=1, keepdims=True),
        jnp.sum(d_acc, axis=1, keepdims=True) + support_energy,
    )
    for i, value in enumerate(locals_):
        tile = jnp.where(column == i, value, tile)

    def reduce_start(stage, value):
        red_out[stage] = value
        return [
            send(red_out.at[stage], red_in.at[15 * stage + i], other)
            for i, other in enumerate(stages[stage])
        ]

    def reduce_finish(stage, copies, value):
        for copy in copies:
            copy.wait()
        for i in range(len(copies)):
            value = value + red_in[15 * stage + i]
        return value

    going = reduce_start(0, tile)
    support_products(term)
    scatter(12, SLOT_PAIRS)
    for k in rim_blocks:
        v_two[k] = assembled(k)
    rims = [
        send(v_two.at[0:EDGE], rim_right.at[1, 0:EDGE], ring(-1)),
        send(v_two.at[ROWS - EDGE : ROWS], rim_left.at[1, 0:EDGE], ring(1)),
    ]
    tile = reduce_finish(0, going, tile)
    going = reduce_start(1, tile)
    for k in inner_blocks:
        v_two[k] = assembled(k)
    for copy in rims:
        copy.wait()
    for k in range(EDGE):
        v_two[EDGE + k] = v_two[EDGE + k] + jnp.where(not_first, rim_left[1, k], 0.0)
        v_two[OWN + k] = v_two[OWN + k] + jnp.where(not_last, rim_right[1, k], 0.0)
    tile = reduce_finish(1, going, tile)
    gamma, a_sum, c_sum, d_sum = [
        jnp.sum(jnp.where(column == i, tile, 0.0), axis=1, keepdims=True) for i in range(4)
    ]
    step_one = gamma / a_sum
    fresh = gamma - 2.0 * step_one * a_sum + step_one * step_one * c_sum
    grow = 1.0 + fresh / gamma
    curve = grow * grow * a_sum - 2.0 * grow * step_one * c_sum + step_one * step_one * d_sum
    step_two = fresh / curve
    along = jnp.broadcast_to(step_one + step_two * grow, (VEC, 128))
    across = jnp.broadcast_to(step_one * step_two, (VEC, 128))
    for k in range(OWN):
        for t in range(2):
            at = slice(128 * t, 128 * t + 128)
            col = slice(LANES * k + 128 * t, LANES * k + 128 * t + 128)
            r = rhs_ref[:, col]
            p = r * row(pre_ref, 2 * k + t)
            sol_ref[:, col] = along * p - across * win[EDGE + k, :, at]
            res_ref[:, col] = r - along * v_one[EDGE + k, :, at] + across * v_two[EDGE + k, :, at]


SENDS = 6 + 2 * 4 + 2 * 2 + 30


def on_device(
    rhs,
    potential,
    precond,
    shift,
    stiffness,
    cell_scale,
    conn,
    cell_count,
    projector,
    support_cell,
    support_atom,
    support_count,
    atom_matrix,
):
    vmem = pl.BlockSpec(memory_space=pltpu.VMEM)
    smem = pl.BlockSpec(memory_space=pltpu.SMEM)
    shape = jax.ShapeDtypeStruct((VEC, NODE_DEV), F32)
    return pl.pallas_call(
        kernel,
        name="pcg",
        out_shape=(shape, shape),
        in_specs=[smem] * 6 + [pl.BlockSpec(memory_space=pltpu.HBM)] * 7,
        out_specs=(vmem, vmem),
        scratch_shapes=[
            pltpu.VMEM((VEC, NODE_DEV), F32),
            pltpu.VMEM((52, 128), F32),
            pltpu.VMEM((52, 128), F32),
            pltpu.VMEM((ELEM, ELEM), F32),
            pltpu.VMEM((CELLS, ELEM), jnp.int32),
            pltpu.VMEM((ENTRIES * NPROJ, ELEM), F32),
            pltpu.VMEM((OWNED * NPROJ, NPROJ), F32),
            pltpu.VMEM((ROWS, VEC, LANES), F32),
            pltpu.VMEM((2, ROWS * VEC, LANES), BF16),
            pltpu.VMEM((4 * EDGE * VEC * 2, LANES), BF16),
            pltpu.VMEM((SLOT_PAIRS, LANES, 2 * PAD), BF16),
            pltpu.VMEM((SLOTS, 1, PAD), jnp.int32),
            pltpu.VMEM((SLOTS, 1, PAD), jnp.int32),
            pltpu.VMEM((SLOTS, 16, PAD), jnp.int16),
            pltpu.VMEM((SLOTS, VEC, PAD), F32),
            pltpu.VMEM((PAIRS, 16, PAD), BF16),
            pltpu.VMEM((PAIRS, 16, PAD), BF16),
            pltpu.VMEM((PAD, PAD), BF16),
            pltpu.VMEM((PAD, PAD), BF16),
            pltpu.VMEM((ENTRIES * NPROJ, PAD), F32),
            pltpu.VMEM((CELLS, PAD), jnp.int32),
            pltpu.VMEM((SLOTS, 16, PAD), BF16),
            pltpu.VMEM((ROWS * 16, LANES), F32),
            pltpu.VMEM((ROWS, VEC, LANES), F32),
            pltpu.VMEM((ROWS, VEC, LANES), F32),
            pltpu.VMEM((2, 2 * EDGE, VEC, LANES), F32),
            pltpu.VMEM((2, 2 * EDGE, VEC, LANES), F32),
            pltpu.VMEM((2, 8, 128), F32),
            pltpu.VMEM((2, 8, 128), F32),
            pltpu.VMEM((2, OWNED * NPROJ, NPROJ), F32),
            pltpu.VMEM((2, 3 * OWNED, VEC, 128), F32),
            pltpu.VMEM((2, 2, VEC, 128), F32),
            pltpu.VMEM((2, 4, VEC, 128), F32),
            pltpu.VMEM((2, 4, VEC, 128), F32),
            pltpu.VMEM((2, 2, VEC, 128), F32),
            pltpu.VMEM((2, VEC, 128), F32),
            pltpu.VMEM((30, VEC, 128), F32),
            pltpu.SemaphoreType.DMA((7,)),
            pltpu.SemaphoreType.DMA((SENDS,)),
            pltpu.SemaphoreType.DMA((SENDS,)),
        ],
        compiler_params=pltpu.CompilerParams(
            collective_id=0, has_side_effects=True, vmem_limit_bytes=32 << 20
        ),
    )(
        cell_count,
        support_cell,
        support_atom,
        support_count,
        shift,
        cell_scale,
        rhs,
        potential.reshape(52, 128),
        precond.reshape(52, 128),
        stiffness,
        conn,
        projector.reshape(ENTRIES * NPROJ, ELEM),
        atom_matrix.reshape(OWNED * NPROJ, NPROJ),
    )


def solution(mesh):
    in_specs = (
        P(None, "dom"),
        P("dom"),
        P("dom"),
        P(),
        P(),
        P("dom"),
        P("dom", None),
        P(),
        P("dom", None, None),
        P("dom"),
        P("dom"),
        P(),
        P("dom", None, None),
    )
    out_specs = (P(None, "dom"), P(None, "dom"))
    return jax.shard_map(
        on_device, mesh=mesh, in_specs=in_specs, out_specs=out_specs, check_vma=False
    )
```

time: 69.4 us -> 54.5 us (0.79)
  the two profiles are of different devices: /device:TPU:8 before, /device:TPU:1 now
where the time goes in v2:
time: 54.5 us; the launch traced here: 54.1 us
  Pallas kernels  45.5 us (83%)
  local copies, waits for them, and re-layouts  7.92 us (15%)
  between operations  0.7 us (1%)
    pallas_call x1, Pallas kernels, on_device(): pl.pallas_call(kernel, name='pcg', out_shape=(shape, shape), in_specs=[sm...  45.5 us
    unnamed x28, local copies, waits for them, and re-layouts  7.92 us

profile of v2, /device:TPU:1, one launch (start us, length us, event | category | flops | bytes accessed | tf_op | source)
XLA Modules:
  0.0 54.1 jit_solution(8998465547633062739)
XLA Ops:
  0.6 0.0 copy-start.12
  0.6 0.0 copy-start.8
  0.7 0.0 copy-start.10
  0.7 0.0 copy-start.11
  0.7 0.0 copy-start.7
  0.7 0.0 copy-start.9
  0.7 0.6 %copy-done.12 = f32[32]{0:T(128)S(1)} copy-done((f32[32]{0:T(128)S(1)}, f32[32]{0:T(128)}, u32[]{:S(2)}) %copy-start.12) | copy-done | bytes 152
  1.3 0.0 copy-done.8
  1.3 0.0 copy-done.10
  1.3 0.0 copy-done.11
  1.3 0.0 copy-done.7
  1.4 0.0 copy-done.9
  1.4 0.0 copy-start
  1.4 1.0 %copy-done = f32[343,343]{1,0:T(8,128)S(1)} copy-done((f32[343,343]{1,0:T(8,128)S(1)}, f32[343,343]{1,0:T(8,128)}, u32[]{:S(2)}) %copy-start) | copy-done | bytes 470620
  2.4 0.0 copy-start.1
  2.4 0.9 %copy-done.1 = f32[8,6656]{1,0:T(8,128)S(1)} copy-done((f32[8,6656]{1,0:T(8,128)S(1)}, f32[8,6656]{1,0:T(8,128)}, u32[]{:S(2)}) %copy-start.1) | copy-done | bytes 213016
  3.4 0.0 copy-start.2
  3.4 0.9 %copy-done.2 = f32[8,8,343]{2,1,0:T(8,128)S(1)} copy-done((f32[8,8,343]{2,1,0:T(8,128)S(1)}, f32[8,8,343]{2,1,0:T(8,128)}, u32[]{:S(2)}) %copy-start.2) | copy-done | bytes 87832
  4.3 0.0 copy-start.3
  4.3 0.8 %copy-done.3 = s32[32,343]{1,0:T(8,128)S(1)} copy-done((s32[32,343]{1,0:T(8,128)S(1)}, s32[32,343]{1,0:T(8,128)}, u32[]{:S(2)}) %copy-start.3) | copy-done | bytes 43928
  5.1 0.0 copy-start.4
  5.1 0.7 %copy-done.4 = f32[6656]{0:T(1024)S(1)} copy-done((f32[6656]{0:T(1024)S(1)}, f32[6656]{0:T(1024)}, u32[]{:S(2)}) %copy-start.4) | copy-done | bytes 26648
  5.8 0.0 copy-start.5
  5.8 0.7 %copy-done.5 = f32[6656]{0:T(1024)S(1)} copy-done((f32[6656]{0:T(1024)S(1)}, f32[6656]{0:T(1024)}, u32[]{:S(2)}) %copy-start.5) | copy-done | bytes 26648
  6.5 0.0 copy-start.6
  6.5 0.7 %copy-done.6 = f32[2,8,8]{2,1,0:T(8,128)S(1)} copy-done((f32[2,8,8]{2,1,0:T(8,128)S(1)}, f32[2,8,8]{2,1,0:T(8,128)}, u32[]{:S(2)}) %copy-start.6) | copy-done | bytes 536
  7.2 45.5 %pcg.1 = (f32[8,6656]{1,0:T(8,128)S(1)}, f32[8,6656]{1,0:T(8,128)S(1)}) custom-call(s32[256]{0:T(256)S(1)} %copy-done.7, s32[8]{0:T(128)S(1)} %copy-done.9, s32[8]{0:T(128)S(1)} %copy-done.10, s32[256]{0:T(256)S(1)} %copy-done.8, f32[8]{0:T(128)S(1)} %copy-done.11, f32[32]{0:T(128)S(1)} %copy-done.12, f32[8,6656]{1,0:T(8,128)S(1)} %copy-done.1, ...), custom_call_target="tpu_custom_call" | custom-call | tf_op jit(solution)/shard_map/pcg/pallas_call | solution.py:558
  52.7 0.7 %copy.20 = f32[8,6656]{1,0:T(8,128)} copy(f32[8,6656]{1,0:T(8,128)S(1)} %get-tuple-element.4) | data formatting | bytes 425984
  53.4 0.7 %copy.21 = f32[8,6656]{1,0:T(8,128)} copy(f32[8,6656]{1,0:T(8,128)S(1)} %get-tuple-element.5) | data formatting | bytes 425984
Async XLA Ops:
  0.6 0.7 %copy-start.12 = (f32[32]{0:T(128)S(1)}, f32[32]{0:T(128)}, u32[]{:S(2)}) copy-start(f32[32]{0:T(128)} %scale_ref.1) | copy-start | bytes 388
  0.6 0.7 %copy-start.8 = (s32[256]{0:T(256)S(1)}, s32[256]{0:T(256)}, u32[]{:S(2)}) copy-start(s32[256]{0:T(256)} %support_count_ref.1) | copy-start | bytes 3076
  0.7 0.7 %copy-start.10 = (s32[8]{0:T(128)S(1)}, s32[8]{0:T(128)}, u32[]{:S(2)}) copy-start(s32[8]{0:T(128)} %support_atom_ref.1) | copy-start | bytes 100
  0.7 0.7 %copy-start.11 = (f32[8]{0:T(128)S(1)}, f32[8]{0:T(128)}, u32[]{:S(2)}) copy-start(f32[8]{0:T(128)} %shift_ref.1) | copy-start | bytes 100
  0.7 0.7 %copy-start.7 = (s32[256]{0:T(256)S(1)}, s32[256]{0:T(256)}, u32[]{:S(2)}) copy-start(s32[256]{0:T(256)} %count_ref.1) | copy-start | bytes 3076
  0.7 0.7 %copy-start.9 = (s32[8]{0:T(128)S(1)}, s32[8]{0:T(128)}, u32[]{:S(2)}) copy-start(s32[8]{0:T(128)} %support_cell_ref.1) | copy-start | bytes 100
  1.4 1.0 %copy-start = (f32[343,343]{1,0:T(8,128)S(1)}, f32[343,343]{1,0:T(8,128)}, u32[]{:S(2)}) copy-start(f32[343,343]{1,0:T(8,128)} %stiff_hbm.1) | copy-start | bytes 1411792
  2.4 0.9 %copy-start.1 = (f32[8,6656]{1,0:T(8,128)S(1)}, f32[8,6656]{1,0:T(8,128)}, u32[]{:S(2)}) copy-start(f32[8,6656]{1,0:T(8,128)} %rhs_hbm.1) | copy-start | bytes 638980
  3.4 0.9 %copy-start.2 = (f32[8,8,343]{2,1,0:T(8,128)S(1)}, f32[8,8,343]{2,1,0:T(8,128)}, u32[]{:S(2)}) copy-start(f32[8,8,343]{2,1,0:T(8,128)} %param.21) | copy-start | bytes 263428
  4.3 0.8 %copy-start.3 = (s32[32,343]{1,0:T(8,128)S(1)}, s32[32,343]{1,0:T(8,128)}, u32[]{:S(2)}) copy-start(s32[32,343]{1,0:T(8,128)} %conn_hbm.1) | copy-start | bytes 131716
  5.1 0.7 %copy-start.4 = (f32[6656]{0:T(1024)S(1)}, f32[6656]{0:T(1024)}, u32[]{:S(2)}) copy-start(f32[6656]{0:T(1024)} %param.14) | copy-start | bytes 79876
  5.8 0.7 %copy-start.5 = (f32[6656]{0:T(1024)S(1)}, f32[6656]{0:T(1024)}, u32[]{:S(2)}) copy-start(f32[6656]{0:T(1024)} %param.15) | copy-start | bytes 79876
  6.5 0.7 %copy-start.6 = (f32[2,8,8]{2,1,0:T(8,128)S(1)}, f32[2,8,8]{2,1,0:T(8,128)}, u32[]{:S(2)}) copy-start(f32[2,8,8]{2,1,0:T(8,128)} %param.25) | copy-start | bytes 1540

commit v3 on v2

--- a/solution.py
+++ b/solution.py
@@ -140,6 +140,9 @@
     def row(ref, index):
         return jnp.broadcast_to(ref[index : index + 1, :], (VEC, 128))
 
+    def wide_row(ref, k):
+        return jnp.concatenate([row(ref, 2 * k), row(ref, 2 * k + 1)], axis=1)
+
     for load in loads[1:4]:
         load.wait()
     dot_acc = jnp.zeros((VEC, 128), F32)
@@ -364,10 +367,27 @@
         stacked = jnp.concatenate(total, axis=0)
         coef = jnp.dot(stacked, fold, precision=HIGH, preferred_element_type=F32)
         coef = jnp.where(same_atom, coef, 0.0)
-        term = jnp.dot(coef, atom_tiled, precision=HIGH, preferred_element_type=F32)
-        both = coef[2 * VEC : 4 * VEC, :] * term[2 * VEC : 4 * VEC, 0:48]
-        energy = jnp.sum(both[0:VEC] + both[VEC : 2 * VEC], axis=1, keepdims=True)
-        return term, energy
+        return jnp.dot(coef, atom_tiled, precision=HIGH, preferred_element_type=F32)
+
+    def own_energy(step, copies):
+        for copy in copies:
+            copy.wait()
+        total = jnp.concatenate(
+            [
+                coef_out[step, OWNED + a, :, 0:64]
+                + coef_m1[step, OWNED + a, :, 0:64]
+                + coef_p1[step, a, :, 0:64]
+                for a in range(OWNED)
+            ],
+            axis=0,
+        )
+        coef = jnp.dot(total, fold[:, 0:16], precision=HIGH, preferred_element_type=F32)
+        coef = jnp.where(same_atom[0:16, 0:16], coef, 0.0)
+        term = jnp.dot(
+            coef, atom_tiled[16:32, :], precision=HIGH, preferred_element_type=F32
+        )
+        both = total * term
+        return jnp.sum(both[0:VEC] + both[VEC : 2 * VEC], axis=1, keepdims=True)
 
     def support_products(term):
         chosen = jnp.zeros((VEC, 64), F32)
@@ -412,7 +432,7 @@
     cell_products()
     acc[...] = jnp.zeros_like(acc)
     scatter(0, PAIRS)
-    term, _ = coef_finish(0, coefs)
+    term = coef_finish(0, coefs)
     support_products(term)
     scatter(PAIRS, SLOT_PAIRS)
     for k in rim_blocks:
@@ -464,13 +484,14 @@
     gather_rim(rim_blocks, 0, PAIRS, True)
     energy = cell_products()
     acc[...] = jnp.zeros_like(acc)
-    scatter(0, 12)
-    term, support_energy = coef_finish(1, coefs)
+    scatter(0, 4)
+    support_energy = own_energy(1, coefs[0:2])
 
     a_acc, c_acc, d_acc = sums
     for t in range(3):
         d_acc = d_acc + energy[:, 128 * t : 128 * t + 128]
     column = lax.broadcasted_iota(jnp.int32, (VEC, 128), 1)
+    place = column - 4 * sublane
     tile = jnp.zeros((VEC, 128), F32)
     locals_ = (
         gamma,
@@ -479,7 +500,8 @@
         jnp.sum(d_acc, axis=1, keepdims=True) + support_energy,
     )
     for i, value in enumerate(locals_):
-        tile = jnp.where(column == i, value, tile)
+        tile = jnp.where(place == i, value, tile)
+    tile = jnp.sum(tile, axis=0, keepdims=True)
 
     def reduce_start(stage, value):
         red_out[stage] = value
@@ -496,8 +518,10 @@
         return value
 
     going = reduce_start(0, tile)
+    scatter(4, PAIRS)
+    term = coef_finish(1, coefs[2:4])
     support_products(term)
-    scatter(12, SLOT_PAIRS)
+    scatter(PAIRS, SLOT_PAIRS)
     for k in rim_blocks:
         v_two[k] = assembled(k)
     rims = [
@@ -515,23 +539,44 @@
         v_two[OWN + k] = v_two[OWN + k] + jnp.where(not_last, rim_right[1, k], 0.0)
     tile = reduce_finish(1, going, tile)
     gamma, a_sum, c_sum, d_sum = [
-        jnp.sum(jnp.where(column == i, tile, 0.0), axis=1, keepdims=True) for i in range(4)
+        jnp.sum(jnp.where(place == i, jnp.broadcast_to(tile, (VEC, 128)), 0.0), axis=1, keepdims=True)
+        for i in range(4)
     ]
     step_one = gamma / a_sum
     fresh = gamma - 2.0 * step_one * a_sum + step_one * step_one * c_sum
     grow = 1.0 + fresh / gamma
     curve = grow * grow * a_sum - 2.0 * grow * step_one * c_sum + step_one * step_one * d_sum
     step_two = fresh / curve
-    along = jnp.broadcast_to(step_one + step_two * grow, (VEC, 128))
-    across = jnp.broadcast_to(step_one * step_two, (VEC, 128))
+    along = jnp.broadcast_to(step_one + step_two * grow, (VEC, LANES))
+    across = jnp.broadcast_to(step_one * step_two, (VEC, LANES))
     for k in range(OWN):
-        for t in range(2):
-            at = slice(128 * t, 128 * t + 128)
-            col = slice(LANES * k + 128 * t, LANES * k + 128 * t + 128)
-            r = rhs_ref[:, col]
-            p = r * row(pre_ref, 2 * k + t)
-            sol_ref[:, col] = along * p - across * win[EDGE + k, :, at]
-            res_ref[:, col] = r - along * v_one[EDGE + k, :, at] + across * v_two[EDGE + k, :, at]
+        r = rhs_ref[:, LANES * k : LANES * k + LANES]
+        image = v_one[EDGE + k]
+        sol_ref[k] = along * (r * wide_row(pre_ref, k)) - across * win[EDGE + k]
+        res_ref[k] = r - along * image + across * v_two[EDGE + k]
+
+
+PARTS = 2
+
+
+def hand_over(answer_ref, left_ref, answer_out, left_out, held, load_sem, store_sem):
+    size = OWN // PARTS
+    loads, stores = [], []
+    for i, (src, dst) in enumerate(((answer_ref, answer_out), (left_ref, left_out))):
+        for p in range(PARTS):
+            piece = pl.ds(size * p, size)
+            at = PARTS * i + p
+            load = pltpu.make_async_copy(src.at[piece], held.at[i, piece], load_sem.at[at])
+            load.start()
+            loads.append(load)
+            stores.append(
+                pltpu.make_async_copy(held.at[i, piece], dst.at[piece], store_sem.at[at])
+            )
+    for load, store in zip(loads, stores):
+        load.wait()
+        store.start()
+    for store in stores:
+        store.wait()
 
 
 SENDS = 6 + 2 * 4 + 2 * 2 + 30
@@ -554,12 +599,13 @@
 ):
     vmem = pl.BlockSpec(memory_space=pltpu.VMEM)
     smem = pl.BlockSpec(memory_space=pltpu.SMEM)
-    shape = jax.ShapeDtypeStruct((VEC, NODE_DEV), F32)
-    return pl.pallas_call(
+    field = jax.ShapeDtypeStruct((OWN, VEC, LANES), F32)
+    anywhere = pl.BlockSpec(memory_space=pl.ANY)
+    answer, left = pl.pallas_call(
         kernel,
         name="pcg",
-        out_shape=(shape, shape),
-        in_specs=[smem] * 6 + [pl.BlockSpec(memory_space=pltpu.HBM)] * 7,
+        out_shape=(field, field),
+        in_specs=[smem] * 6 + [anywhere] * 7,
         out_specs=(vmem, vmem),
         scratch_shapes=[
             pltpu.VMEM((VEC, NODE_DEV), F32),
@@ -597,14 +643,14 @@
             pltpu.VMEM((2, 4, VEC, 128), F32),
             pltpu.VMEM((2, 4, VEC, 128), F32),
             pltpu.VMEM((2, 2, VEC, 128), F32),
-            pltpu.VMEM((2, VEC, 128), F32),
-            pltpu.VMEM((30, VEC, 128), F32),
+            pltpu.VMEM((2, 1, 128), F32),
+            pltpu.VMEM((30, 1, 128), F32),
             pltpu.SemaphoreType.DMA((7,)),
             pltpu.SemaphoreType.DMA((SENDS,)),
             pltpu.SemaphoreType.DMA((SENDS,)),
         ],
         compiler_params=pltpu.CompilerParams(
-            collective_id=0, has_side_effects=True, vmem_limit_bytes=32 << 20
+            collective_id=0, has_side_effects=True, vmem_limit_bytes=60 << 20
         ),
     )(
         cell_count,
@@ -621,6 +667,25 @@
         projector.reshape(ENTRIES * NPROJ, ELEM),
         atom_matrix.reshape(OWNED * NPROJ, NPROJ),
     )
+
+    answer, left = pl.pallas_call(
+        hand_over,
+        name="hand_over",
+        out_shape=(field, field),
+        in_specs=[anywhere] * 2,
+        out_specs=(anywhere, anywhere),
+        scratch_shapes=[
+            pltpu.VMEM((2, OWN, VEC, LANES), F32),
+            pltpu.SemaphoreType.DMA((2 * PARTS,)),
+            pltpu.SemaphoreType.DMA((2 * PARTS,)),
+        ],
+        compiler_params=pltpu.CompilerParams(vmem_limit_bytes=60 << 20),
+    )(answer, left)
+
+    def rows(blocks):
+        return jnp.transpose(blocks, (1, 0, 2)).reshape(VEC, NODE_DEV)
+
+    return (rows(answer), rows(left))
 
 
 def solution(mesh):

time: 54.5 us -> 48.2 us (0.88)
  local copies, waits for them, and re-layouts: 7.92 us -> 0 us
  Pallas kernels: 45.5 us -> 46.7 us
    unnamed x28 -> x0, local copies, waits for them, and re-layouts: 7.92 us -> none
    pallas_call x1 -> x2, Pallas kernels: 45.5 us -> 46.7 us  [the longest x1 44.9 us: on_device(): pl.pallas_call(kernel, name='pcg', out_shape=(field, field), in_specs=[sm...]
where the time goes in v3:
time: 48.2 us; the launch traced here: 47.3 us
  Pallas kernels  46.7 us (97%)
  between operations  0.64 us (1%)
    pallas_call x1, Pallas kernels, on_device(): pl.pallas_call(kernel, name='pcg', out_shape=(field, field), in_specs=[sm...  44.9 us
    pallas_call x1, Pallas kernels, on_device(): pl.pallas_call(hand_over, name='hand_over', out_shape=(field, field), in_...  1.76 us

profile of v3, /device:TPU:1, one launch (start us, length us, event | category | flops | bytes accessed | tf_op | source)
XLA Modules:
  0.0 47.3 jit_solution(13568668752045812368)
XLA Ops:
  0.6 44.9 %pcg.1 = (f32[26,8,256]{2,1,0:T(8,128)}, f32[26,8,256]{2,1,0:T(8,128)}) custom-call(s32[256]{0:T(256)} %count_ref.1, s32[8]{0:T(128)} %support_cell_ref.1, s32[8]{0:T(128)} %support_atom_ref.1, s32[256]{0:T(256)} %support_count_ref.1, f32[8]{0:T(128)} %shift_ref.1, f32[32]{0:T(128)} %scale_ref.1, f32[8,6656]{1,0:T(8,128)} %rhs_hbm.1, f32[52,128]{1,0:T(8,128)} %bitcast.11, ...), custom_call_target="tpu_custom_call" | custom-call | tf_op jit(solution)/shard_map/pcg/pallas_call | solution.py:604
  45.5 1.8 %hand_over.1 = (f32[26,8,256]{2,1,0:T(8,128)}, f32[26,8,256]{2,1,0:T(8,128)}) custom-call(f32[26,8,256]{2,1,0:T(8,128)} %get-tuple-element.6.answer_ref, f32[26,8,256]{2,1,0:T(8,128)} %get-tuple-element.7.left_ref), custom_call_target="tpu_custom_call" | custom-call | tf_op jit(solution)/shard_map/hand_over/pallas_call | solution.py:671

commit v4 on v3

--- a/solution.py
+++ b/solution.py
@@ -102,7 +102,7 @@
     for group in stages:
         greeted = greeted + group
     barrier = pltpu.get_barrier_semaphore()
-    for other in greeted:
+    for other in greeted[0:4]:
         pl.semaphore_signal(barrier, inc=1, device_id=(other,), device_id_type=MESH)
 
     loads = []
@@ -120,6 +120,9 @@
         load = pltpu.make_async_copy(src, dst, load_sem.at[i])
         load.start()
         loads.append(load)
+
+    for other in greeted[4:]:
+        pl.semaphore_signal(barrier, inc=1, device_id=(other,), device_id_type=MESH)
 
     used = [0]
 
@@ -224,7 +227,7 @@
                     values[2 * c + q, :, 128 * t : 128 * t + 128] = got
             return carry
 
-        lax.fori_loop(0, SLOT_PAIRS, body, 0, unroll=4)
+        lax.fori_loop(0, SLOT_PAIRS, body, 0, unroll=10)
 
     def prepare_rim(blocks):
         count = len(blocks) * VEC
@@ -262,7 +265,7 @@
                 lhs_lo[c] = jnp.concatenate(downs, axis=0)
             return carry
 
-        lax.fori_loop(first_pair, last_pair, body, 0, unroll=4)
+        lax.fori_loop(first_pair, last_pair, body, 0, unroll=last_pair - first_pair)
 
     def scatter(first_pair, last_pair):
         def body(c, carry):
@@ -275,7 +278,7 @@
             )
             return carry
 
-        lax.fori_loop(first_pair, last_pair, body, 0, unroll=4)
+        lax.fori_loop(first_pair, last_pair, body, 0, unroll=last_pair - first_pair)
 
     own_blocks = list(range(EDGE, EDGE + OWN))
     ghost_blocks = list(range(EDGE)) + list(range(EDGE + OWN, ROWS))
@@ -296,6 +299,7 @@
 
     lane64 = lax.broadcasted_iota(jnp.int32, (1, 64), 1)
     entry_of = jnp.right_shift(lane64, 3)
+    channel_of = jnp.bitwise_and(lane64, 7)
     live_entries = support_count_ref[me]
     atom_row = jnp.full((1, 64), -1, jnp.int32)
     relative = []
@@ -307,9 +311,6 @@
     shift_col = jnp.zeros((VEC, 128), F32)
     for v in range(VEC):
         shift_col = jnp.where(sublane == v, shift_ref[v], shift_col)
-    r64 = lax.broadcasted_iota(jnp.int32, (64, 48), 0)
-    c48 = lax.broadcasted_iota(jnp.int32, (64, 48), 1)
-    fold = jnp.where(jnp.bitwise_and(r64, 7) == jnp.bitwise_and(c48, 7), 1.0, 0.0).astype(F32)
     r48 = lax.broadcasted_iota(jnp.int32, (48, 48), 0)
     d48 = lax.broadcasted_iota(jnp.int32, (48, 48), 1)
     same_atom = jnp.right_shift(r48, 3) == jnp.right_shift(d48, 3)
@@ -327,17 +328,14 @@
     atom_tiled = jnp.dot(atoms, tile8, precision=HIGH, preferred_element_type=F32)
 
     def coef_start(step):
-        picked = values[CELLS:SLOTS].reshape(ENTRIES * VEC, PAD)
-        cross = lax.dot_general(
-            picked,
-            proj_pad[...],
-            (((1,), (1,)), ((), ())),
-            precision=HIGH,
-            preferred_element_type=F32,
-        )
         own = [jnp.zeros((VEC, 64), F32) for _ in range(3 * OWNED)]
         for s in range(ENTRIES):
-            mine = jnp.where(entry_of == s, cross[VEC * s : VEC * s + VEC, :], 0.0)
+            field = values[CELLS + s]
+            mine = jnp.zeros((VEC, 64), F32)
+            for j in range(NPROJ):
+                at = NPROJ * s + j
+                sums = jnp.sum(field * proj_pad[at : at + 1, :], axis=1, keepdims=True)
+                mine = jnp.where(channel_of == j, sums, mine)
             for a in range(3 * OWNED):
                 own[a] = own[a] + jnp.where(relative[s] == a, mine, 0.0)
         for a in range(3 * OWNED):
@@ -365,8 +363,7 @@
             own[5] + right1[3] + right2[1],
         ]
         stacked = jnp.concatenate(total, axis=0)
-        coef = jnp.dot(stacked, fold, precision=HIGH, preferred_element_type=F32)
-        coef = jnp.where(same_atom, coef, 0.0)
+        coef = jnp.where(same_atom, stacked[:, 0:48], 0.0)
         return jnp.dot(coef, atom_tiled, precision=HIGH, preferred_element_type=F32)
 
     def own_energy(step, copies):
@@ -381,12 +378,11 @@
             ],
             axis=0,
         )
-        coef = jnp.dot(total, fold[:, 0:16], precision=HIGH, preferred_element_type=F32)
-        coef = jnp.where(same_atom[0:16, 0:16], coef, 0.0)
+        coef = jnp.where(same_atom[0:16, 0:16], total[:, 0:16], 0.0)
         term = jnp.dot(
             coef, atom_tiled[16:32, :], precision=HIGH, preferred_element_type=F32
         )
-        both = total * term
+        both = jnp.where(lane64 < NPROJ, total * term, 0.0)
         return jnp.sum(both[0:VEC] + both[VEC : 2 * VEC], axis=1, keepdims=True)
 
     def support_products(term):
@@ -559,24 +555,17 @@
 PARTS = 2
 
 
-def hand_over(answer_ref, left_ref, answer_out, left_out, held, load_sem, store_sem):
+def hand_over(answer_ref, left_ref, answer_out, left_out, sem):
+    copies = []
     size = OWN // PARTS
-    loads, stores = [], []
     for i, (src, dst) in enumerate(((answer_ref, answer_out), (left_ref, left_out))):
         for p in range(PARTS):
             piece = pl.ds(size * p, size)
-            at = PARTS * i + p
-            load = pltpu.make_async_copy(src.at[piece], held.at[i, piece], load_sem.at[at])
-            load.start()
-            loads.append(load)
-            stores.append(
-                pltpu.make_async_copy(held.at[i, piece], dst.at[piece], store_sem.at[at])
-            )
-    for load, store in zip(loads, stores):
-        load.wait()
-        store.start()
-    for store in stores:
-        store.wait()
+            copy = pltpu.make_async_copy(src.at[piece], dst.at[piece], sem.at[PARTS * i + p])
+            copy.start()
+            copies.append(copy)
+    for copy in copies:
+        copy.wait()
 
 
 SENDS = 6 + 2 * 4 + 2 * 2 + 30
@@ -650,37 +639,35 @@
             pltpu.SemaphoreType.DMA((SENDS,)),
         ],
         compiler_params=pltpu.CompilerParams(
-            collective_id=0, has_side_effects=True, vmem_limit_bytes=60 << 20
+            collective_id=0, has_side_effects=True, vmem_limit_bytes=40 << 20
         ),
     )(
-        cell_count,
-        support_cell,
-        support_atom,
-        support_count,
-        shift,
-        cell_scale,
-        rhs,
-        potential.reshape(52, 128),
-        precond.reshape(52, 128),
-        stiffness,
-        conn,
-        projector.reshape(ENTRIES * NPROJ, ELEM),
-        atom_matrix.reshape(OWNED * NPROJ, NPROJ),
+        pltpu.with_memory_space_constraint(cell_count, pltpu.HBM),
+        pltpu.with_memory_space_constraint(support_cell, pltpu.HBM),
+        pltpu.with_memory_space_constraint(support_atom, pltpu.HBM),
+        pltpu.with_memory_space_constraint(support_count, pltpu.HBM),
+        pltpu.with_memory_space_constraint(shift, pltpu.HBM),
+        pltpu.with_memory_space_constraint(cell_scale, pltpu.HBM),
+        pltpu.with_memory_space_constraint(rhs, pltpu.HBM),
+        pltpu.with_memory_space_constraint(potential.reshape(52, 128), pltpu.HBM),
+        pltpu.with_memory_space_constraint(precond.reshape(52, 128), pltpu.HBM),
+        pltpu.with_memory_space_constraint(stiffness, pltpu.HBM),
+        pltpu.with_memory_space_constraint(conn, pltpu.HBM),
+        pltpu.with_memory_space_constraint(projector.reshape(ENTRIES * NPROJ, ELEM), pltpu.HBM),
+        pltpu.with_memory_space_constraint(atom_matrix.reshape(OWNED * NPROJ, NPROJ), pltpu.HBM),
     )
 
     answer, left = pl.pallas_call(
         hand_over,
         name="hand_over",
         out_shape=(field, field),
-        in_specs=[anywhere] * 2,
+        in_specs=[vmem] * 2,
         out_specs=(anywhere, anywhere),
-        scratch_shapes=[
-            pltpu.VMEM((2, OWN, VEC, LANES), F32),
-            pltpu.SemaphoreType.DMA((2 * PARTS,)),
-            pltpu.SemaphoreType.DMA((2 * PARTS,)),
-        ],
-        compiler_params=pltpu.CompilerParams(vmem_limit_bytes=60 << 20),
-    )(answer, left)
+        scratch_shapes=[pltpu.SemaphoreType.DMA((2 * PARTS,))],
+    )(
+        pltpu.with_memory_space_constraint(answer, pltpu.VMEM),
+        pltpu.with_memory_space_constraint(left, pltpu.VMEM),
+    )
 
     def rows(blocks):
         return jnp.transpose(blocks, (1, 0, 2)).reshape(VEC, NODE_DEV)

time: 48.2 us -> 46.3 us (0.961)
  the two profiles are of different devices: /device:TPU:1 before, /device:TPU:0 now
where the time goes in v4:
time: 46.3 us; the launch traced here: 46.1 us
  Pallas kernels  45.3 us (98%)
  between operations  0.8 us (2%)
    pallas_call x1, Pallas kernels, on_device(): pl.pallas_call(kernel, name='pcg', out_shape=(field, field), in_specs=[sm...  44.6 us

profile of v4, /device:TPU:0, one launch (start us, length us, event | category | flops | bytes accessed | tf_op | source)
XLA Modules:
  0.0 46.1 jit_solution(2473112849834901634)
XLA Ops:
  0.6 44.6 %pcg.1 = (f32[26,8,256]{2,1,0:T(8,128)S(1)}, f32[26,8,256]{2,1,0:T(8,128)S(1)}) custom-call(s32[256]{0:T(256)} %count_ref.1, s32[8]{0:T(128)} %support_cell_ref.1, s32[8]{0:T(128)} %support_atom_ref.1, s32[256]{0:T(256)} %support_count_ref.1, f32[8]{0:T(128)} %shift_ref.1, f32[32]{0:T(128)} %scale_ref.1, f32[8,6656]{1,0:T(8,128)} %rhs_hbm.1, ...), custom_call_target="tpu_custom_call" | custom-call | tf_op jit(solution)/shard_map/pcg/pallas_call | solution.py:593
  45.2 0.8 %hand_over.1 = (f32[26,8,256]{2,1,0:T(8,128)}, f32[26,8,256]{2,1,0:T(8,128)}) custom-call(f32[26,8,256]{2,1,0:T(8,128)S(1)} %get-tuple-element.6.answer_ref, f32[26,8,256]{2,1,0:T(8,128)S(1)} %get-tuple-element.7.left_ref), custom_call_target="tpu_custom_call" | custom-call | tf_op jit(solution)/shard_map/hand_over/pallas_call | solution.py:660

commit v5 on v4

--- a/solution.py
+++ b/solution.py
@@ -140,6 +140,34 @@
         copy.start()
         return copy
 
+    class RingCopy:
+        def __init__(self, src, dst, step):
+            slot = used[0]
+            used[0] = slot + 1
+            self.copy = pltpu.make_async_remote_copy(
+                src_ref=src,
+                dst_ref=dst,
+                send_sem=send_sem.at[slot],
+                recv_sem=recv_sem.at[slot],
+                device_id=(ring(step),),
+                device_id_type=MESH,
+            )
+            self.sends = me >= -step if step < 0 else me < N_DOM - step
+            self.receives = me < N_DOM + step if step < 0 else me >= step
+
+            @pl.when(self.sends)
+            def _():
+                self.copy.start()
+
+        def wait(self):
+            @pl.when(self.sends)
+            def _():
+                self.copy.wait_send()
+
+            @pl.when(self.receives)
+            def _():
+                self.copy.wait_recv()
+
     def row(ref, index):
         return jnp.broadcast_to(ref[index : index + 1, :], (VEC, 128))
 
@@ -162,12 +190,12 @@
     pre_out[1, 0:4, :] = pre_ref[48:52, :]
     pl.semaphore_wait(barrier, len(greeted))
     first = [
-        send(win.at[EDGE : 2 * EDGE], win.at[ROWS - EDGE : ROWS], ring(-1)),
-        send(win.at[OWN : OWN + EDGE], win.at[0:EDGE], ring(1)),
-        send(pre_out.at[0], pre_in.at[1], ring(-1)),
-        send(pre_out.at[1], pre_in.at[0], ring(1)),
-        send(atom_ref, atom_in.at[1], ring(-1)),
-        send(atom_ref, atom_in.at[0], ring(1)),
+        RingCopy(win.at[EDGE : 2 * EDGE], win.at[ROWS - EDGE : ROWS], -1),
+        RingCopy(win.at[OWN : OWN + EDGE], win.at[0:EDGE], 1),
+        RingCopy(pre_out.at[0], pre_in.at[1], -1),
+        RingCopy(pre_out.at[1], pre_in.at[0], 1),
+        RingCopy(atom_ref, atom_in.at[1], -1),
+        RingCopy(atom_ref, atom_in.at[0], 1),
     ]
 
     loads[0].wait()
@@ -299,7 +327,9 @@
 
     lane64 = lax.broadcasted_iota(jnp.int32, (1, 64), 1)
     entry_of = jnp.right_shift(lane64, 3)
-    channel_of = jnp.bitwise_and(lane64, 7)
+    lane128 = lax.broadcasted_iota(jnp.int32, (1, 128), 1)
+    channel_of = jnp.bitwise_and(lane128, 7)
+    group_of = jnp.right_shift(lane128, 3)
     live_entries = support_count_ref[me]
     atom_row = jnp.full((1, 64), -1, jnp.int32)
     relative = []
@@ -311,12 +341,11 @@
     shift_col = jnp.zeros((VEC, 128), F32)
     for v in range(VEC):
         shift_col = jnp.where(sublane == v, shift_ref[v], shift_col)
-    r48 = lax.broadcasted_iota(jnp.int32, (48, 48), 0)
-    d48 = lax.broadcasted_iota(jnp.int32, (48, 48), 1)
-    same_atom = jnp.right_shift(r48, 3) == jnp.right_shift(d48, 3)
     r8 = lax.broadcasted_iota(jnp.int32, (8, 64), 0)
     c64 = lax.broadcasted_iota(jnp.int32, (8, 64), 1)
     tile8 = jnp.where(r8 == jnp.bitwise_and(c64, 7), 1.0, 0.0).astype(F32)
+    row_atom = jnp.right_shift(lax.broadcasted_iota(jnp.int32, (48, 64), 0), 3)
+    column_atom = jnp.right_shift(lax.broadcasted_iota(jnp.int32, (48, 48), 1), 3)
     for copy in first:
         copy.wait()
     not_first = me > 0
@@ -324,71 +353,58 @@
     for k in range(EDGE):
         win[k] = jnp.where(not_first, win[k], 0.0)
         win[ROWS - EDGE + k] = jnp.where(not_last, win[ROWS - EDGE + k], 0.0)
-    atoms = jnp.concatenate([atom_in[0], atom_ref[...], atom_in[1]], axis=0)
+    atoms_left = jnp.where(not_first, atom_in[0], 0.0)
+    atoms_right = jnp.where(not_last, atom_in[1], 0.0)
+    atoms = jnp.concatenate([atoms_left, atom_ref[...], atoms_right], axis=0)
     atom_tiled = jnp.dot(atoms, tile8, precision=HIGH, preferred_element_type=F32)
+    entry_atoms = jnp.where(row_atom == atom_row, atom_tiled, 0.0)
+    owned_column = (column_atom >= OWNED) & (column_atom < 2 * OWNED)
+    diagonal_block = (row_atom[:, 0:48] == column_atom) & owned_column
+    own_atoms = jnp.where(diagonal_block, atom_tiled[:, 0:48], 0.0)
 
     def coef_start(step):
-        own = [jnp.zeros((VEC, 64), F32) for _ in range(3 * OWNED)]
+        own = jnp.zeros((VEC, 128), F32)
         for s in range(ENTRIES):
             field = values[CELLS + s]
-            mine = jnp.zeros((VEC, 64), F32)
+            mine = jnp.zeros((VEC, 128), F32)
             for j in range(NPROJ):
                 at = NPROJ * s + j
                 sums = jnp.sum(field * proj_pad[at : at + 1, :], axis=1, keepdims=True)
                 mine = jnp.where(channel_of == j, sums, mine)
-            for a in range(3 * OWNED):
-                own[a] = own[a] + jnp.where(relative[s] == a, mine, 0.0)
-        for a in range(3 * OWNED):
-            coef_out[step, a, :, 0:64] = own[a]
+            own = own + jnp.where(group_of == relative[s], mine, 0.0)
+        coef_out[step] = own
         copies = [
-            send(coef_out.at[step, 0:4], coef_p1.at[step], ring(-1)),
-            send(coef_out.at[step, 2:6], coef_m1.at[step], ring(1)),
-            send(coef_out.at[step, 0:2], coef_p2.at[step], ring(-2)),
-            send(coef_out.at[step, 4:6], coef_m2.at[step], ring(2)),
+            RingCopy(coef_out.at[step], coef_p1.at[step], -1),
+            RingCopy(coef_out.at[step], coef_m1.at[step], 1),
+            RingCopy(coef_out.at[step], coef_p2.at[step], -2),
+            RingCopy(coef_out.at[step], coef_m2.at[step], 2),
         ]
         return copies
+
+    def moved(tile, blocks):
+        return pltpu.roll(tile, (128 - 16 * blocks) % 128, axis=1)
+
+    def near_sum(step):
+        left = jnp.where(not_first, coef_m1[step], 0.0)
+        right = jnp.where(not_last, coef_p1[step], 0.0)
+        return coef_out[step] + moved(left, 1) + moved(right, -1)
 
     def coef_finish(step, copies):
         for copy in copies:
             copy.wait()
-        own = coef_out[step, :, :, 0:64]
-        left2, left1 = coef_m2[step, :, :, 0:64], coef_m1[step, :, :, 0:64]
-        right1, right2 = coef_p1[step, :, :, 0:64], coef_p2[step, :, :, 0:64]
-        total = [
-            own[0] + left1[0] + left2[0],
-            own[1] + left1[1] + left2[1],
-            own[2] + left1[2] + right1[0],
-            own[3] + left1[3] + right1[1],
-            own[4] + right1[2] + right2[0],
-            own[5] + right1[3] + right2[1],
-        ]
-        stacked = jnp.concatenate(total, axis=0)
-        coef = jnp.where(same_atom, stacked[:, 0:48], 0.0)
-        return jnp.dot(coef, atom_tiled, precision=HIGH, preferred_element_type=F32)
+        left = jnp.where(me > 1, coef_m2[step], 0.0)
+        right = jnp.where(me < N_DOM - 2, coef_p2[step], 0.0)
+        total = near_sum(step) + moved(left, 2) + moved(right, -2)
+        return jnp.dot(total[:, 0:48], entry_atoms, precision=HIGH, preferred_element_type=F32)
 
     def own_energy(step, copies):
         for copy in copies:
             copy.wait()
-        total = jnp.concatenate(
-            [
-                coef_out[step, OWNED + a, :, 0:64]
-                + coef_m1[step, OWNED + a, :, 0:64]
-                + coef_p1[step, a, :, 0:64]
-                for a in range(OWNED)
-            ],
-            axis=0,
-        )
-        coef = jnp.where(same_atom[0:16, 0:16], total[:, 0:16], 0.0)
-        term = jnp.dot(
-            coef, atom_tiled[16:32, :], precision=HIGH, preferred_element_type=F32
-        )
-        both = jnp.where(lane64 < NPROJ, total * term, 0.0)
-        return jnp.sum(both[0:VEC] + both[VEC : 2 * VEC], axis=1, keepdims=True)
-
-    def support_products(term):
-        chosen = jnp.zeros((VEC, 64), F32)
-        for a in range(3 * OWNED):
-            chosen = chosen + jnp.where(atom_row == a, term[VEC * a : VEC * a + VEC, :], 0.0)
+        total = near_sum(step)[:, 0:48]
+        applied = jnp.dot(total, own_atoms, precision=HIGH, preferred_element_type=F32)
+        return jnp.sum(total * applied, axis=1, keepdims=True)
+
+    def support_products(chosen):
         back = jnp.concatenate(
             [jnp.where(entry_of == s, chosen, 0.0) for s in range(ENTRIES)], axis=0
         )
@@ -434,8 +450,8 @@
     for k in rim_blocks:
         v_one[k] = assembled(k)
     rims = [
-        send(v_one.at[0 : 2 * EDGE], rim_right.at[0], ring(-1)),
-        send(v_one.at[OWN:ROWS], rim_left.at[0], ring(1)),
+        RingCopy(v_one.at[0 : 2 * EDGE], rim_right.at[0], -1),
+        RingCopy(v_one.at[OWN:ROWS], rim_left.at[0], 1),
     ]
     for k in inner_blocks:
         v_one[k] = assembled(k)
@@ -480,7 +496,7 @@
     gather_rim(rim_blocks, 0, PAIRS, True)
     energy = cell_products()
     acc[...] = jnp.zeros_like(acc)
-    scatter(0, 4)
+    scatter(0, 8)
     support_energy = own_energy(1, coefs[0:2])
 
     a_acc, c_acc, d_acc = sums
@@ -514,15 +530,15 @@
         return value
 
     going = reduce_start(0, tile)
-    scatter(4, PAIRS)
+    scatter(8, PAIRS)
     term = coef_finish(1, coefs[2:4])
     support_products(term)
     scatter(PAIRS, SLOT_PAIRS)
     for k in rim_blocks:
         v_two[k] = assembled(k)
     rims = [
-        send(v_two.at[0:EDGE], rim_right.at[1, 0:EDGE], ring(-1)),
-        send(v_two.at[ROWS - EDGE : ROWS], rim_left.at[1, 0:EDGE], ring(1)),
+        RingCopy(v_two.at[0:EDGE], rim_right.at[1, 0:EDGE], -1),
+        RingCopy(v_two.at[ROWS - EDGE : ROWS], rim_left.at[1, 0:EDGE], 1),
     ]
     tile = reduce_finish(0, going, tile)
     going = reduce_start(1, tile)
@@ -627,11 +643,11 @@
             pltpu.VMEM((2, 8, 128), F32),
             pltpu.VMEM((2, 8, 128), F32),
             pltpu.VMEM((2, OWNED * NPROJ, NPROJ), F32),
-            pltpu.VMEM((2, 3 * OWNED, VEC, 128), F32),
-            pltpu.VMEM((2, 2, VEC, 128), F32),
-            pltpu.VMEM((2, 4, VEC, 128), F32),
-            pltpu.VMEM((2, 4, VEC, 128), F32),
-            pltpu.VMEM((2, 2, VEC, 128), F32),
+            pltpu.VMEM((2, VEC, 128), F32),
+            pltpu.VMEM((2, VEC, 128), F32),
+            pltpu.VMEM((2, VEC, 128), F32),
+            pltpu.VMEM((2, VEC, 128), F32),
+            pltpu.VMEM((2, VEC, 128), F32),
             pltpu.VMEM((2, 1, 128), F32),
             pltpu.VMEM((30, 1, 128), F32),
             pltpu.SemaphoreType.DMA((7,)),

time: 46.3 us -> 45.1 us (0.974)
  the two profiles are of different devices: /device:TPU:0 before, /device:TPU:1 now
where the time goes in v5:
time: 45.1 us; the launch traced here: 45 us
  Pallas kernels  44.2 us (98%)
  between operations  0.8 us (2%)
    pallas_call x1, Pallas kernels, on_device(): pl.pallas_call(kernel, name='pcg', out_shape=(field, field), in_specs=[sm...  43.4 us

profile of v5, /device:TPU:1, one launch (start us, length us, event | category | flops | bytes accessed | tf_op | source)
XLA Modules:
  0.0 45.0 jit_solution(12456834294447916865)
XLA Ops:
  0.6 43.4 %pcg.1 = (f32[26,8,256]{2,1,0:T(8,128)S(1)}, f32[26,8,256]{2,1,0:T(8,128)S(1)}) custom-call(s32[256]{0:T(256)} %count_ref.1, s32[8]{0:T(128)} %support_cell_ref.1, s32[8]{0:T(128)} %support_atom_ref.1, s32[256]{0:T(256)} %support_count_ref.1, f32[8]{0:T(128)} %shift_ref.1, f32[32]{0:T(128)} %scale_ref.1, f32[8,6656]{1,0:T(8,128)} %rhs_hbm.1, ...), custom_call_target="tpu_custom_call" | custom-call | tf_op jit(solution)/shard_map/pcg/pallas_call | solution.py:609
  44.0 0.8 %hand_over.1 = (f32[26,8,256]{2,1,0:T(8,128)}, f32[26,8,256]{2,1,0:T(8,128)}) custom-call(f32[26,8,256]{2,1,0:T(8,128)S(1)} %get-tuple-element.6.answer_ref, f32[26,8,256]{2,1,0:T(8,128)S(1)} %get-tuple-element.7.left_ref), custom_call_target="tpu_custom_call" | custom-call | tf_op jit(solution)/shard_map/hand_over/pallas_call | solution.py:676

commit v6 on v5

--- a/solution.py
+++ b/solution.py
@@ -496,8 +496,7 @@
     gather_rim(rim_blocks, 0, PAIRS, True)
     energy = cell_products()
     acc[...] = jnp.zeros_like(acc)
-    scatter(0, 8)
-    support_energy = own_energy(1, coefs[0:2])
+    scatter(0, 4)
 
     a_acc, c_acc, d_acc = sums
     for t in range(3):
@@ -509,10 +508,11 @@
         gamma,
         jnp.sum(a_acc, axis=1, keepdims=True),
         jnp.sum(c_acc, axis=1, keepdims=True),
-        jnp.sum(d_acc, axis=1, keepdims=True) + support_energy,
+        jnp.sum(d_acc, axis=1, keepdims=True),
     )
     for i, value in enumerate(locals_):
         tile = jnp.where(place == i, value, tile)
+    tile = tile + jnp.where(place == 3, own_energy(1, coefs[0:2]), 0.0)
     tile = jnp.sum(tile, axis=0, keepdims=True)
 
     def reduce_start(stage, value):
@@ -530,7 +530,7 @@
         return value
 
     going = reduce_start(0, tile)
-    scatter(8, PAIRS)
+    scatter(4, PAIRS)
     term = coef_finish(1, coefs[2:4])
     support_products(term)
     scatter(PAIRS, SLOT_PAIRS)

time: 45.1 us -> 43.9 us (0.973)
  Pallas kernels: 44.2 us -> 42.7 us
    pallas_call x1, Pallas kernels: 43.4 us -> 41.9 us  [on_device(): pl.pallas_call(kernel, name='pcg', out_shape=(field, field), in_specs=[sm...]
where the time goes in v6:
time: 43.9 us; the launch traced here: 43.5 us
  Pallas kernels  42.7 us (97%)
  between operations  0.8 us (2%)
    pallas_call x1, Pallas kernels, on_device(): pl.pallas_call(kernel, name='pcg', out_shape=(field, field), in_specs=[sm...  41.9 us

profile of v6, /device:TPU:1, one launch (start us, length us, event | category | flops | bytes accessed | tf_op | source)
XLA Modules:
  0.0 43.5 jit_solution(7270904037830227757)
XLA Ops:
  0.6 41.9 %pcg.1 = (f32[26,8,256]{2,1,0:T(8,128)S(1)}, f32[26,8,256]{2,1,0:T(8,128)S(1)}) custom-call(s32[256]{0:T(256)} %count_ref.1, s32[8]{0:T(128)} %support_cell_ref.1, s32[8]{0:T(128)} %support_atom_ref.1, s32[256]{0:T(256)} %support_count_ref.1, f32[8]{0:T(128)} %shift_ref.1, f32[32]{0:T(128)} %scale_ref.1, f32[8,6656]{1,0:T(8,128)} %rhs_hbm.1, ...), custom_call_target="tpu_custom_call" | custom-call | tf_op jit(solution)/shard_map/pcg/pallas_call | solution.py:609
  42.5 0.8 %hand_over.1 = (f32[26,8,256]{2,1,0:T(8,128)}, f32[26,8,256]{2,1,0:T(8,128)}) custom-call(f32[26,8,256]{2,1,0:T(8,128)S(1)} %get-tuple-element.6.answer_ref, f32[26,8,256]{2,1,0:T(8,128)S(1)} %get-tuple-element.7.left_ref), custom_call_target="tpu_custom_call" | custom-call | tf_op jit(solution)/shard_map/hand_over/pallas_call | solution.py:676
